TPU v7x, 256 devices: a whole 4x4x8 slice. The times are simulated.
256 devices in a mesh: gx: 8 (over x, core), gy: 4 (over y), gz: 8 (over z).
Axes of the slice: x: 4, y: 4, z: 8, core: 2. Of those that a mesh axis runs over, the one named last changes fastest.
Arguments:
- segments: float32 [16384, 12, 128], P(('gx', 'gy', 'gz')), may hold values from -8 to 8, as said below
- remesh_matrix: float32 [128, 128], replicated, may hold values from -1 to 2, as said below
- ghost_list: int32 [256, 8, 4], P(('gx', 'gy', 'gz')), may hold values from 0 to 63
- pair_list: int32 [256, 512, 2], P(('gx', 'gy', 'gz')), may hold values from 0 to 159, as said below
- tile_count: int32 [256], P(('gx', 'gy', 'gz')), may hold values from 128 to 512, as said below
- cut_axis: int32 [3], replicated, may hold values from 0 to 2, each once
- mig_list: int32 [256, 3, 24], P(('gx', 'gy', 'gz')), may hold values from 0 to 63, as said below
- mig_count: int32 [256, 3], P(('gx', 'gy', 'gz')), may hold values from 8 to 24
Outputs:
- segments_out: float32 [16384, 12, 128], P(('gx', 'gy', 'gz'))
Inputs may be any that keep to these rules, and one draw needn't show every extreme that they name: `segments`: components 0-2 and 3-5 are real values, 6-8 smaller ones, and 9-11 lie between 0.3 and 3. `remesh_matrix`: A dominant diagonal near 0.7 with dense independent entries beside it. `pair_list`: the first entry of a row is one of the domain's own blocks, below 64; the second indexes the domain's own blocks followed by its 96 ghost blocks. `tile_count`: in every draw some domain uses all 512 rows. `cut_axis`: each of the three directions is cut at exactly one step. `mig_list`: the entries of one domain's list for one step differ from each other.
All inputs are finite; a program needn't handle non-finite values.
Results may differ from a plain program's by a relative error of at most 0.00055.
Values sent between devices are 32-bit elements; how exact they have to be, the bound alone decides.
A program may use at most 64 MiB of HBM per device.

v0:
```python
import functools

import jax
import jax.numpy as jnp
from jax import lax
from jax.experimental import pallas as pl
from jax.experimental.pallas import tpu as pltpu
from jax.sharding import PartitionSpec as P

STEPS = 3
MESH = pl.DeviceIdType.MESH

core_square = 0.1
time_step = 0.5
stress_coef = 0.25

GROUP = 16


def layout_of(tiles, blocks, ghosts, slots):
    sizes = dict(
        target=tiles,
        source=tiles,
        term=tiles,
        keep=tiles,
        last=blocks,
        ghost=ghosts,
        mig=STEPS * slots,
        rank=STEPS * blocks,
        cut=STEPS,
        count=STEPS,
    )
    offsets, total = {}, 0
    for name, size in sizes.items():
        offsets[name] = total
        total += size
    return offsets, total


def index_table(ghost_list, pair_list, tile_count, cut_axis, mig_list, mig_count, blocks, sources):
    tiles = pair_list.shape[1]
    targets, origin = pair_list[0, :, 0], pair_list[0, :, 1]
    number = jnp.arange(tiles, dtype=jnp.int32)
    dead = (number >= tile_count[0]).astype(jnp.int32)
    key = targets * tiles + number
    place = jnp.sum((key[None, :] < key[:, None]).astype(jnp.int32), axis=1)
    packed = (targets * 1024 + origin) * 2 + dead
    hit = place[None, :] == number[:, None]
    ordered = jnp.sum(jnp.where(hit, packed[None, :], 0), axis=1)
    target = ordered // 2048
    source = (ordered // 2) % 1024
    term = jnp.where(ordered % 2 == 1, sources, source)
    before = jnp.concatenate([jnp.full((1,), -1, jnp.int32), target[:-1]])
    keep = (target == before).astype(jnp.int32)
    slot = jnp.arange(blocks, dtype=jnp.int32)
    upto = jnp.sum((targets[None, :] <= slot[:, None]).astype(jnp.int32), axis=1)
    own = jnp.sum((targets[None, :] == slot[:, None]).astype(jnp.int32), axis=1)
    last = jnp.where(own > 0, upto - 1, tiles)
    lists = mig_list[0]
    capacity = lists.shape[1]
    match = lists[:, None, :] == slot[None, :, None]
    order = jnp.arange(capacity, dtype=jnp.int32)
    rank = jnp.min(jnp.where(match, order[None, None, :], capacity), axis=2)
    return jnp.concatenate(
        [
            target,
            source,
            term,
            keep,
            last,
            ghost_list[0].reshape(-1),
            lists.reshape(-1),
            rank.reshape(-1),
            cut_axis,
            mig_count[0],
        ]
    )


def kernel(
    at,
    sizes,
    table,
    segments,
    matrix,
    result,
    geo,
    inv,
    own,
    src,
    terms,
    spread,
    sums,
    field,
    got,
    ghost_out,
    ghost_in,
    inv_out,
    inv_in,
    geo_out,
    geo_in,
    ghost_send,
    ghost_recv,
    inv_send,
    inv_recv,
    geo_send,
    geo_recv,
):
    blocks, tiles, ghosts, capacity = sizes
    width = segments.shape[2]
    here = tuple(lax.axis_index(name) for name in ("gx", "gy", "gz"))

    def shifted(axis, by):
        count = lax.axis_size(("gx", "gy", "gz")[axis])
        place = list(here)
        place[axis] = lax.rem(here[axis] + (by % count), count)
        return tuple(place)

    neighbours = []
    for axis in range(3):
        neighbours += [shifted(axis, 1), shifted(axis, -1)]
    partners = [
        shifted(axis, lax.axis_size(name) // 2) for axis, name in enumerate(("gx", "gy", "gz"))
    ]

    barrier = pltpu.get_barrier_semaphore()
    for device in neighbours + partners:
        pl.semaphore_signal(barrier, inc=1, device_id=device, device_id_type=MESH)

    row = lax.broadcasted_iota(jnp.int32, (8, width), 0)

    def rows(ref, i, count=8):
        return ref[pl.ds(i, count, stride=blocks), :]

    def load_state(i, carry):
        block = segments[i]
        geo[pl.ds(i, 3, stride=blocks), :] = block[0:3]
        geo[pl.ds(3 * blocks + i, 3, stride=blocks), :] = block[6:9]
        inv[pl.ds(i, 3, stride=blocks), :] = block[9:12]
        inv[pl.ds(3 * blocks + i, 3, stride=blocks), :] = block[3:6]
        return carry

    geo[6 * blocks : 8 * blocks, :] = jnp.zeros((2 * blocks, width), jnp.float32)
    inv[6 * blocks : 8 * blocks, :] = jnp.zeros((2 * blocks, width), jnp.float32)
    lax.fori_loop(0, blocks, load_state, 0, unroll=8)
    terms[blocks + ghosts] = jnp.zeros((8, width), jnp.float32)
    sums[tiles] = jnp.zeros((8, width), jnp.float32)
    pl.semaphore_wait(barrier, 9)

    def products(block):
        first = jnp.where(
            row >= 6, pltpu.roll(block, 3, 0), jnp.where(row == 2, pltpu.roll(block, 7, 0), block)
        )
        second = jnp.where(
            row >= 6, pltpu.roll(block, 2, 0), jnp.where(row == 2, pltpu.roll(block, 5, 0), block)
        )
        second = jnp.where(
            (row >= 3) & (row < 6), block, second
        )
        return first * second

    def ghost_copy(s, face):
        axis, low = face // 2, face % 2
        octants = ghost_out.at[s]
        bit = 1 - low
        part = (octants.at[bit], octants.at[:, bit], octants.at[:, :, bit])[axis]
        return pltpu.make_async_remote_copy(
            src_ref=part,
            dst_ref=ghost_in.at[s, face],
            send_sem=ghost_send.at[s, face],
            recv_sem=ghost_recv.at[s, face],
            device_id=neighbours[face],
            device_id_type=MESH,
        )

    def partner_copy(source, landing, send, recv, s, axis):
        return pltpu.make_async_remote_copy(
            src_ref=source.at[s],
            dst_ref=landing.at[s, axis],
            send_sem=send.at[s, axis],
            recv_sem=recv.at[s, axis],
            device_id=partners[axis],
            device_id_type=MESH,
        )

    def step(s, carry):
        def own_block(i, c):
            block = jnp.where(row < 3, rows(geo, i), rows(inv, i))
            own[i] = block
            src[i] = block
            terms[i] = products(block)
            return c

        lax.fori_loop(0, blocks, own_block, 0, unroll=8)

        for o in range(8):
            for q in range(4):
                pick = table[at["ghost"] + o * 4 + q]
                ghost_out[s, o // 4, (o // 2) % 2, o % 2, q] = own[pick]
        for face in range(6):
            ghost_copy(s, face).start()

        my_count = table[at["count"] + s].astype(jnp.float32)

        def out_inv(r, c):
            slot = table[at["mig"] + s * capacity + r]
            inv_out[s, r] = rows(inv, slot)
            return c

        lax.fori_loop(0, capacity, out_inv, 0, unroll=8)
        inv_out[s, capacity] = jnp.full((8, width), my_count, jnp.float32)
        for axis in range(3):
            partner_copy(inv_out, inv_in, inv_send, inv_recv, s, axis).start()

        def spread_block(i, c):
            turned = own[i].T
            for k in range(3):
                spread[i, k] = jnp.broadcast_to(turned[:, k : k + 1], (width, width))
            return c

        lax.fori_loop(0, blocks, spread_block, 0, unroll=4)

        for face in range(6):
            ghost_copy(s, face).wait_recv()

            def ghost_block(q, c, face=face):
                for u in range(4):
                    block = ghost_in[s, face, q // 2, q % 2, u]
                    spot = blocks + face * 16 + q * 4 + u
                    src[spot] = block
                    terms[spot] = products(block)
                return c

            lax.fori_loop(0, 4, ghost_block, 0, unroll=2)

        def tile_group(g, run):
            for u in range(0, GROUP, 2):
                weights, factors = [], []
                for v in range(2):
                    t = g * GROUP + u + v
                    i, j = table[at["target"] + t], table[at["source"] + t]
                    squared = None
                    for k in range(3):
                        offset = spread[i, k] - src[j, pl.ds(k, 1), :]
                        offset = offset * offset
                        squared = offset if squared is None else squared + offset
                    weights.append((1.0 / (squared + core_square)).astype(jnp.bfloat16))
                    factors.append(terms[table[at["term"] + t]])
                both = lax.dot_general(
                    jnp.concatenate(factors, axis=0).astype(jnp.bfloat16),
                    jnp.concatenate(weights, axis=0),
                    (((1,), (1,)), ((), ())),
                    preferred_element_type=jnp.float32,
                )
                for v in range(2):
                    t = g * GROUP + u + v
                    part = both[8 * v : 8 * v + 8, v * width : (v + 1) * width]
                    run = jnp.where(table[at["keep"] + t] != 0, run, 0.0) + part
                    sums[t] = run
            return run

        lax.fori_loop(0, tiles // GROUP, tile_group, jnp.zeros((8, width), jnp.float32))

        def collect(i, c):
            field[pl.ds(i, 8, stride=blocks), :] = sums[table[at["last"] + i]]
            return c

        lax.fori_loop(0, blocks, collect, 0, unroll=8)

        def comp(ref, k):
            return ref[k * blocks : (k + 1) * blocks, :]

        scale = stress_coef / width
        sxx, syy, szz = (comp(field, k) * scale for k in (3, 4, 5))
        sxy, syz, sxz = (comp(field, k) * scale for k in (6, 7, 2))
        b = [comp(inv, k) for k in (3, 4, 5)]
        force = (
            sxx * b[0] + sxy * b[1] + sxz * b[2],
            sxy * b[0] + syy * b[1] + syz * b[2],
            sxz * b[0] + syz * b[1] + szz * b[2],
        )
        for k in range(3):
            velocity = comp(inv, k) * force[k]
            previous = comp(geo, 3 + k)
            geo[k * blocks : (k + 1) * blocks, :] = comp(geo, k) + time_step * (
                1.5 * velocity - 0.5 * previous
            )
            geo[(3 + k) * blocks : (4 + k) * blocks, :] = velocity
        geo[0 : 3 * blocks, :] = jnp.dot(
            geo[0 : 3 * blocks, :],
            matrix[...],
            precision=lax.Precision.HIGHEST,
            preferred_element_type=jnp.float32,
        )

        def out_geo(r, c):
            slot = table[at["mig"] + s * capacity + r]
            geo_out[s, r] = rows(geo, slot)
            return c

        lax.fori_loop(0, capacity, out_geo, 0, unroll=8)
        for axis in range(3):
            partner_copy(geo_out, geo_in, geo_send, geo_recv, s, axis).start()
        for axis in range(3):
            partner_copy(inv_out, inv_in, inv_send, inv_recv, s, axis).wait_recv()
        cut = table[at["cut"] + s]

        def chosen(landing, r):
            later = jnp.where(cut == 1, landing[s, 1, r], landing[s, 2, r])
            return jnp.where(cut == 0, landing[s, 0, r], later)

        limit = jnp.minimum(chosen(inv_in, capacity), my_count)

        def take(ref, landing):
            def gather(r, c):
                got[r] = chosen(landing, r)
                return c

            lax.fori_loop(0, capacity, gather, 0, unroll=8)

            def body(i, c):
                r = table[at["rank"] + s * blocks + i]
                arrived = got[jnp.minimum(r, capacity - 1)]
                live = limit > r.astype(jnp.float32)
                ref[pl.ds(i, 8, stride=blocks), :] = jnp.where(live, arrived, rows(ref, i))
                return c

            lax.fori_loop(0, blocks, body, 0, unroll=8)

        take(inv, inv_in)
        for axis in range(3):
            partner_copy(geo_out, geo_in, geo_send, geo_recv, s, axis).wait_recv()
        take(geo, geo_in)
        for face in range(6):
            ghost_copy(s, face).wait_send()
        for axis in range(3):
            partner_copy(inv_out, inv_in, inv_send, inv_recv, s, axis).wait_send()
            partner_copy(geo_out, geo_in, geo_send, geo_recv, s, axis).wait_send()
        return carry

    lax.fori_loop(0, STEPS, step, 0)

    def store_state(i, carry):
        g, v = rows(geo, i), rows(inv, i)
        result[i, 0:3, :] = g[0:3]
        result[i, 3:6, :] = v[3:6]
        result[i, 6:9, :] = g[3:6]
        result[i, 9:12, :] = v[0:3]
        return carry

    lax.fori_loop(0, blocks, store_state, 0, unroll=8)


def on_device(
    segments, remesh_matrix, ghost_list, pair_list, tile_count, cut_axis, mig_list, mig_count
):
    blocks, _, width = segments.shape
    tiles = pair_list.shape[1]
    per_cell = ghost_list.shape[2]
    ghosts = 24 * per_cell
    capacity = mig_list.shape[2]
    at, _ = layout_of(tiles, blocks, 8 * per_cell, capacity)
    table = index_table(
        ghost_list, pair_list, tile_count, cut_axis, mig_list, mig_count, blocks, blocks + ghosts
    )
    vmem = pl.BlockSpec(memory_space=pltpu.VMEM)
    f32 = jnp.float32
    return pl.pallas_call(
        functools.partial(kernel, at, (blocks, tiles, ghosts, capacity)),
        out_shape=jax.ShapeDtypeStruct(segments.shape, f32),
        in_specs=[pl.BlockSpec(memory_space=pltpu.SMEM), vmem, vmem],
        out_specs=vmem,
        scratch_shapes=[
            pltpu.VMEM((8 * blocks, width), f32),
            pltpu.VMEM((8 * blocks, width), f32),
            pltpu.VMEM((blocks, 8, width), f32),
            pltpu.VMEM((blocks + ghosts, 8, width), f32),
            pltpu.VMEM((blocks + ghosts + 1, 8, width), f32),
            pltpu.VMEM((blocks, 3, width, width), f32),
            pltpu.VMEM((tiles + 1, 8, width), f32),
            pltpu.VMEM((8 * blocks, width), f32),
            pltpu.VMEM((capacity, 8, width), f32),
            pltpu.VMEM((STEPS, 2, 2, 2, per_cell, 8, width), f32),
            pltpu.VMEM((STEPS, 6, 2, 2, per_cell, 8, width), f32),
            pltpu.VMEM((STEPS, capacity + 1, 8, width), f32),
            pltpu.VMEM((STEPS, 3, capacity + 1, 8, width), f32),
            pltpu.VMEM((STEPS, capacity, 8, width), f32),
            pltpu.VMEM((STEPS, 3, capacity, 8, width), f32),
            pltpu.SemaphoreType.DMA((STEPS, 6)),
            pltpu.SemaphoreType.DMA((STEPS, 6)),
            pltpu.SemaphoreType.DMA((STEPS, 3)),
            pltpu.SemaphoreType.DMA((STEPS, 3)),
            pltpu.SemaphoreType.DMA((STEPS, 3)),
            pltpu.SemaphoreType.DMA((STEPS, 3)),
        ],
        compiler_params=pltpu.CompilerParams(
            collective_id=0, has_side_effects=True, vmem_limit_bytes=48 * 1024 * 1024
        ),
    )(table, segments, remesh_matrix)


def solution(mesh):
    return jax.shard_map(
        on_device,
        mesh=mesh,
        in_specs=(
            P(("gx", "gy", "gz"), None, None),
            P(),
            P(("gx", "gy", "gz"), None, None),
            P(("gx", "gy", "gz"), None, None),
            P(("gx", "gy", "gz")),
            P(),
            P(("gx", "gy", "gz"), None, None),
            P(("gx", "gy", "gz"), None),
        ),
        out_specs=P(("gx", "gy", "gz"), None, None),
        check_vma=False,
    )
```

profile of v0, /device:TPU:2, one launch (start us, length us, event | category | flops | bytes accessed | tf_op | source)
XLA Modules:
  0.0 109.9 jit_solution(4396463126168661280)
XLA Ops:
  0.7 0.0 copy-start.1
  0.7 0.7 copy-done.1
  1.3 0.1 select_reduce_fusion.1
  1.4 0.1 reshape.41
  1.5 0.0 copy-start.3
  1.5 0.1 reshape_squeeze.7
  1.6 0.6 copy-done.3
  2.2 0.0 copy-start.2
  2.2 0.1 copy.15
  2.3 0.1 reshape_squeeze.6
  2.4 0.5 copy-done.2
  2.9 0.1 convert_reduce_fusion.1
  3.1 0.2 convert_reduce_fusion
  3.3 0.2 select_reduce_fusion
  3.5 0.0 copy-start.4
  3.5 0.0 copy-start.5
  3.6 0.1 fusion.3
  3.6 0.6 copy-done.4
  4.2 0.0 copy-done.5
  4.2 0.1 concatenate.7.table
  4.3 0.0 copy-start
  4.3 1.3 %copy.16.segments = f32[64,12,128]{2,1,0:T(8,128)S(1)} copy(f32[64,12,128]{2,0,1:T(8,128)} %param.8) | data formatting | bytes 786432 | tf_op args[0]
  5.6 0.0 copy-done
  5.6 103.5 %shard_map.82 = f32[64,12,128]{2,1,0:T(8,128)S(1)} custom-call(s32[2414]{0:T(1024)S(1)} %concatenate.7.table, f32[64,12,128]{2,1,0:T(8,128)S(1)} %copy.16.segments, f32[128,128]{1,0:T(8,128)S(1)} %copy-done), custom_call_target="tpu_custom_call" | custom-call | tf_op jit(solution)/shard_map/pallas_call | solution.py:368
  109.0 0.9 copy.17
  (6 shorter events, 0.1 us)
Async XLA Ops:
  0.7 0.7 copy-start.1
  1.5 0.7 copy-start.3
  2.2 0.7 copy-start.2
  3.5 0.7 copy-start.4
  3.5 0.7 copy-start.5
  4.3 1.3 %copy-start = (f32[128,128]{1,0:T(8,128)S(1)}, f32[128,128]{1,0:T(8,128)}, u32[]{:S(2)}) copy-start(f32[128,128]{1,0:T(8,128)} %matrix.1) | copy-start | bytes 196612
where the time goes:
time: 111 us; the launch traced here: 110 us
  Pallas kernels  103 us (93%)
  local copies, waits for them, and re-layouts  4.93 us (4%)
    pallas_call x1, Pallas kernels, on_device(): pl.pallas_call(functools.partial(kernel, at, (blocks, tiles, ghosts, capa...  103 us
    unnamed x15, local copies, waits for them, and re-layouts  3.72 us

commit v1 on v0

--- a/solution.py
+++ b/solution.py
@@ -87,9 +87,11 @@
     geo,
     inv,
     own,
-    src,
+    near,
+    far,
     terms,
-    spread,
+    weights_a,
+    weights_b,
     sums,
     field,
     got,
@@ -145,6 +147,7 @@
     lax.fori_loop(0, blocks, load_state, 0, unroll=8)
     terms[blocks + ghosts] = jnp.zeros((8, width), jnp.float32)
     sums[tiles] = jnp.zeros((8, width), jnp.float32)
+    weights_b[...] = jnp.zeros_like(weights_b)
     pl.semaphore_wait(barrier, 9)
 
     def products(block):
@@ -158,6 +161,39 @@
             (row >= 3) & (row < 6), block, second
         )
         return first * second
+
+    def features(block, target):
+        place = jnp.where(row < 3, block, 0.0)
+        square = place * place
+        norm = pltpu.roll(square, 3, 0) + pltpu.roll(square, 2, 0) + pltpu.roll(square, 1, 0)
+        if target:
+            place, norm = -2.0 * place, norm + core_square
+        whole = jnp.where(row == 3, norm, place)
+        high = whole.astype(jnp.bfloat16).astype(jnp.float32)
+        rest = whole - high
+        middle = rest.astype(jnp.bfloat16).astype(jnp.float32)
+        low = rest - middle
+        upper = row < 4
+        edge = (row == 3) | (row == 7)
+        high_up, middle_up = pltpu.roll(high, 4, 0), pltpu.roll(middle, 4, 0)
+        mixed = jnp.where(upper, high, middle_up)
+        if target:
+            low_up = pltpu.roll(low, 4, 0)
+            parts = [
+                mixed,
+                jnp.where(row == 7, 1.0, jnp.where(upper, low, high_up)),
+                jnp.where(edge, 1.0, mixed),
+                jnp.where(edge, 0.0, jnp.where(upper, middle, low_up)),
+            ]
+        else:
+            small = jnp.where(upper, low, middle_up)
+            parts = [
+                jnp.where(edge, 1.0, jnp.where(upper, high, high_up)),
+                jnp.where(row == 3, 1.0, mixed),
+                jnp.where(row == 7, high_up, small),
+                small,
+            ]
+        return jnp.concatenate(parts, axis=0).astype(jnp.bfloat16)
 
     def ghost_copy(s, face):
         axis, low = face // 2, face % 2
@@ -187,7 +223,8 @@
         def own_block(i, c):
             block = jnp.where(row < 3, rows(geo, i), rows(inv, i))
             own[i] = block
-            src[i] = block
+            near[i] = features(block, True)
+            far[i] = features(block, False).T
             terms[i] = products(block)
             return c
 
@@ -212,14 +249,6 @@
         for axis in range(3):
             partner_copy(inv_out, inv_in, inv_send, inv_recv, s, axis).start()
 
-        def spread_block(i, c):
-            turned = own[i].T
-            for k in range(3):
-                spread[i, k] = jnp.broadcast_to(turned[:, k : k + 1], (width, width))
-            return c
-
-        lax.fori_loop(0, blocks, spread_block, 0, unroll=4)
-
         for face in range(6):
             ghost_copy(s, face).wait_recv()
 
@@ -227,39 +256,54 @@
                 for u in range(4):
                     block = ghost_in[s, face, q // 2, q % 2, u]
                     spot = blocks + face * 16 + q * 4 + u
-                    src[spot] = block
+                    far[spot] = features(block, False).T
                     terms[spot] = products(block)
                 return c
 
             lax.fori_loop(0, 4, ghost_block, 0, unroll=2)
 
-        def tile_group(g, run):
+        def weigh(t, out):
+            product = jnp.dot(
+                far[table[at["source"] + t]],
+                near[table[at["target"] + t]],
+                preferred_element_type=jnp.float32,
+            )
+            out[...] = (1.0 / jnp.maximum(product, core_square)).astype(jnp.bfloat16)
+
+        blank = jnp.zeros((8, width), jnp.float32)
+
+        def add_pair(t, weights, u, run):
+            first = terms[table[at["term"] + t]]
+            second = terms[table[at["term"] + t + 1]]
+            left = jnp.concatenate([first, blank], axis=0)
+            right = jnp.concatenate([blank, second], axis=0)
+            both = jnp.dot(
+                jnp.concatenate([left, right], axis=1).astype(jnp.bfloat16),
+                jnp.concatenate([weights[u], weights[u + 1]], axis=0),
+                preferred_element_type=jnp.float32,
+            )
+            for v in range(2):
+                run = jnp.where(table[at["keep"] + t + v] != 0, run, 0.0) + both[8 * v : 8 * v + 8]
+                sums[t + v] = run
+            return run
+
+        groups = tiles // GROUP
+
+        def half(g, run, fill, ready):
+            past = lax.rem(g + groups - 1, groups)
             for u in range(0, GROUP, 2):
-                weights, factors = [], []
                 for v in range(2):
-                    t = g * GROUP + u + v
-                    i, j = table[at["target"] + t], table[at["source"] + t]
-                    squared = None
-                    for k in range(3):
-                        offset = spread[i, k] - src[j, pl.ds(k, 1), :]
-                        offset = offset * offset
-                        squared = offset if squared is None else squared + offset
-                    weights.append((1.0 / (squared + core_square)).astype(jnp.bfloat16))
-                    factors.append(terms[table[at["term"] + t]])
-                both = lax.dot_general(
-                    jnp.concatenate(factors, axis=0).astype(jnp.bfloat16),
-                    jnp.concatenate(weights, axis=0),
-                    (((1,), (1,)), ((), ())),
-                    preferred_element_type=jnp.float32,
-                )
-                for v in range(2):
-                    t = g * GROUP + u + v
-                    part = both[8 * v : 8 * v + 8, v * width : (v + 1) * width]
-                    run = jnp.where(table[at["keep"] + t] != 0, run, 0.0) + part
-                    sums[t] = run
+                    weigh(g * GROUP + u + v, fill.at[u + v])
+                run = add_pair(past * GROUP + u, ready, u, run)
             return run
 
-        lax.fori_loop(0, tiles // GROUP, tile_group, jnp.zeros((8, width), jnp.float32))
+        def two_groups(h, run):
+            run = half(2 * h, run, weights_a, weights_b)
+            return half(2 * h + 1, run, weights_b, weights_a)
+
+        run = lax.fori_loop(0, groups // 2, two_groups, blank)
+        for u in range(0, GROUP, 2):
+            run = add_pair((groups - 1) * GROUP + u, weights_b, u, run)
 
         def collect(i, c):
             field[pl.ds(i, 8, stride=blocks), :] = sums[table[at["last"] + i]]
@@ -364,7 +408,7 @@
         ghost_list, pair_list, tile_count, cut_axis, mig_list, mig_count, blocks, blocks + ghosts
     )
     vmem = pl.BlockSpec(memory_space=pltpu.VMEM)
-    f32 = jnp.float32
+    f32, bf16 = jnp.float32, jnp.bfloat16
     return pl.pallas_call(
         functools.partial(kernel, at, (blocks, tiles, ghosts, capacity)),
         out_shape=jax.ShapeDtypeStruct(segments.shape, f32),
@@ -374,9 +418,11 @@
             pltpu.VMEM((8 * blocks, width), f32),
             pltpu.VMEM((8 * blocks, width), f32),
             pltpu.VMEM((blocks, 8, width), f32),
-            pltpu.VMEM((blocks + ghosts, 8, width), f32),
+            pltpu.VMEM((blocks, 32, width), bf16),
+            pltpu.VMEM((blocks + ghosts, width, 32), bf16),
             pltpu.VMEM((blocks + ghosts + 1, 8, width), f32),
-            pltpu.VMEM((blocks, 3, width, width), f32),
+            pltpu.VMEM((GROUP, width, width), bf16),
+            pltpu.VMEM((GROUP, width, width), bf16),
             pltpu.VMEM((tiles + 1, 8, width), f32),
             pltpu.VMEM((8 * blocks, width), f32),
             pltpu.VMEM((capacity, 8, width), f32),

time: 111 us -> 88.3 us (0.80)
  the two profiles are of different devices: /device:TPU:2 before, /device:TPU:25 now
where the time goes in v1:
time: 88.3 us; the launch traced here: 88.1 us
  Pallas kernels  81.6 us (92%)
  local copies, waits for them, and re-layouts  4.93 us (6%)
    pallas_call x1, Pallas kernels, on_device(): pl.pallas_call(functools.partial(kernel, at, (blocks, tiles, ghosts, capa...  81.6 us
    unnamed x15, local copies, waits for them, and re-layouts  3.72 us

profile of v1, /device:TPU:25, one launch (start us, length us, event | category | flops | bytes accessed | tf_op | source)
XLA Modules:
  0.0 88.1 jit_solution(2834394020878905613)
XLA Ops:
  0.7 0.0 copy-start.1
  0.7 0.7 copy-done.1
  1.3 0.1 select_reduce_fusion.1
  1.4 0.1 reshape.41
  1.5 0.0 copy-start.3
  1.5 0.1 reshape_squeeze.7
  1.6 0.6 copy-done.3
  2.2 0.0 copy-start.2
  2.2 0.1 copy.15
  2.3 0.1 reshape_squeeze.6
  2.4 0.5 copy-done.2
  2.9 0.1 convert_reduce_fusion.1
  3.1 0.2 convert_reduce_fusion
  3.3 0.2 select_reduce_fusion
  3.5 0.0 copy-start.4
  3.5 0.0 copy-start.5
  3.6 0.1 fusion.3
  3.6 0.6 copy-done.4
  4.2 0.0 copy-done.5
  4.2 0.1 concatenate.7.table
  4.3 0.0 copy-start
  4.3 1.3 %copy.16.segments = f32[64,12,128]{2,1,0:T(8,128)S(1)} copy(f32[64,12,128]{2,0,1:T(8,128)} %param.8) | data formatting | bytes 786432 | tf_op args[0]
  5.6 0.0 copy-done
  5.6 81.6 %shard_map.82 = f32[64,12,128]{2,1,0:T(8,128)S(1)} custom-call(s32[2414]{0:T(1024)S(1)} %concatenate.7.table, f32[64,12,128]{2,1,0:T(8,128)S(1)} %copy.16.segments, f32[128,128]{1,0:T(8,128)S(1)} %copy-done), custom_call_target="tpu_custom_call" | custom-call | tf_op jit(solution)/shard_map/pallas_call | solution.py:412
  87.2 0.9 copy.17
  (6 shorter events, 0.1 us)
Async XLA Ops:
  0.7 0.7 copy-start.1
  1.5 0.7 copy-start.3
  2.2 0.7 copy-start.2
  3.5 0.7 copy-start.4
  3.5 0.7 copy-start.5
  4.3 1.3 %copy-start = (f32[128,128]{1,0:T(8,128)S(1)}, f32[128,128]{1,0:T(8,128)}, u32[]{:S(2)}) copy-start(f32[128,128]{1,0:T(8,128)} %matrix.1) | copy-start | bytes 196612

commit v2 on v1

v2 whole, which is shorter than its diff:
```python
import functools

import jax
import jax.numpy as jnp
from jax import lax
from jax.experimental import pallas as pl
from jax.experimental.pallas import tpu as pltpu
from jax.sharding import PartitionSpec as P

STEPS = 3
MESH = pl.DeviceIdType.MESH

core_square = 0.1
time_step = 0.5
stress_coef = 0.25

GROUP = 16


def layout_of(tiles, blocks, ghosts, slots):
    sizes = dict(
        target=tiles,
        source=tiles,
        term=tiles,
        keep=tiles,
        last=blocks,
        ghost=ghosts,
        mig=STEPS * slots,
        rank=STEPS * blocks,
        cut=STEPS,
        count=STEPS,
    )
    offsets, total = {}, 0
    for name, size in sizes.items():
        offsets[name] = total
        total += size
    return offsets, total


def index_table(ghost_list, pair_list, tile_count, cut_axis, mig_list, mig_count, blocks, ghosts):
    tiles = pair_list.shape[1]
    lists = mig_list[0]
    capacity = lists.shape[1]
    targets, origin = pair_list[0, :, 0], pair_list[0, :, 1]
    number = jnp.arange(tiles, dtype=jnp.int32)
    dead = (number >= tile_count[0]).astype(jnp.int32)
    key = targets * tiles + number
    place = jnp.sum((key[None, :] < key[:, None]).astype(jnp.int32), axis=1)
    packed = (targets * 1024 + origin) * 2 + dead
    hit = place[None, :] == number[:, None]
    ordered = jnp.sum(jnp.where(hit, packed[None, :], 0), axis=1)
    target = ordered // 2048
    source = (ordered // 2) % 1024
    source = jnp.where(source < blocks, source, source + capacity)
    term = jnp.where(ordered % 2 == 1, blocks + capacity + ghosts, source)
    before = jnp.concatenate([jnp.full((1,), -1, jnp.int32), target[:-1]])
    keep = (target == before).astype(jnp.int32)
    slot = jnp.arange(blocks, dtype=jnp.int32)
    upto = jnp.sum((targets[None, :] <= slot[:, None]).astype(jnp.int32), axis=1)
    own = jnp.sum((targets[None, :] == slot[:, None]).astype(jnp.int32), axis=1)
    last = jnp.where(own > 0, upto - 1, tiles)
    match = lists[:, None, :] == slot[None, :, None]
    order = jnp.arange(capacity, dtype=jnp.int32)
    rank = jnp.min(jnp.where(match, order[None, None, :], capacity), axis=2)
    return jnp.concatenate(
        [
            target,
            source,
            term,
            keep,
            last,
            ghost_list[0].reshape(-1),
            lists.reshape(-1),
            rank.reshape(-1),
            cut_axis,
            mig_count[0],
        ]
    )


def kernel(
    at,
    sizes,
    table,
    segments,
    matrix,
    result,
    geo,
    inv,
    own,
    near,
    far,
    terms,
    weights_a,
    weights_b,
    sums,
    field,
    remap,
    counts,
    count_out,
    count_in,
    ghost_out,
    ghost_in,
    inv_out,
    inv_in,
    pos_out,
    pos_in,
    vel_out,
    vel_in,
    inv_got,
    pos_got,
    vel_got,
    count_local,
    count_send,
    count_recv,
    ghost_send,
    ghost_recv,
    inv_send,
    inv_recv,
    pos_send,
    pos_recv,
    vel_send,
    vel_recv,
):
    blocks, tiles, ghosts, capacity = sizes
    width = segments.shape[2]
    held = blocks + capacity
    here = tuple(lax.axis_index(name) for name in ("gx", "gy", "gz"))

    def shifted(axis, by):
        count = lax.axis_size(("gx", "gy", "gz")[axis])
        place = list(here)
        place[axis] = lax.rem(here[axis] + (by % count), count)
        return tuple(place)

    neighbours = []
    for axis in range(3):
        neighbours += [shifted(axis, 1), shifted(axis, -1)]
    partners = [
        shifted(axis, lax.axis_size(name) // 2) for axis, name in enumerate(("gx", "gy", "gz"))
    ]

    barrier = pltpu.get_barrier_semaphore()
    for device in neighbours + partners:
        pl.semaphore_signal(barrier, inc=1, device_id=device, device_id_type=MESH)

    row = lax.broadcasted_iota(jnp.int32, (8, width), 0)
    blank = jnp.zeros((8, width), jnp.float32)

    def rows(ref, i, stride=blocks, count=8):
        return ref[pl.ds(i, count, stride=stride), :]

    def remote(source, landing, send, recv, device):
        return pltpu.make_async_remote_copy(
            src_ref=source,
            dst_ref=landing,
            send_sem=send,
            recv_sem=recv,
            device_id=device,
            device_id_type=MESH,
        )

    def load_state(i, carry):
        block = segments[i]
        geo[pl.ds(i, 3, stride=blocks), :] = block[0:3]
        geo[pl.ds(3 * blocks + i, 3, stride=blocks), :] = block[6:9]
        inv[pl.ds(i, 3, stride=blocks), :] = block[9:12]
        inv[pl.ds(3 * blocks + i, 3, stride=blocks), :] = block[3:6]
        own[i] = block[0:8]
        return carry

    geo[6 * blocks : 8 * blocks, :] = jnp.zeros((2 * blocks, width), jnp.float32)
    inv[6 * blocks : 8 * blocks, :] = jnp.zeros((2 * blocks, width), jnp.float32)
    lax.fori_loop(0, blocks, load_state, 0, unroll=8)
    terms[held + ghosts] = blank
    sums[tiles] = blank
    weights_b[...] = jnp.zeros_like(weights_b)
    for ref in (inv_got, pos_got, vel_got):
        ref[...] = jnp.zeros_like(ref)

    def plain(i, carry):
        remap[i] = i
        return carry

    lax.fori_loop(0, held + ghosts + 1, plain, 0)
    for s in range(STEPS):
        count_out[s] = jnp.full((8, width), table[at["count"] + s], jnp.int32)
    pl.semaphore_wait(barrier, 9)

    def products(block):
        first = jnp.where(
            row >= 6, pltpu.roll(block, 3, 0), jnp.where(row == 2, pltpu.roll(block, 7, 0), block)
        )
        second = jnp.where(
            row >= 6, pltpu.roll(block, 2, 0), jnp.where(row == 2, pltpu.roll(block, 5, 0), block)
        )
        return first * second

    def features(block, target):
        place = jnp.where(row < 3, block, 0.0)
        square = place * place
        norm = pltpu.roll(square, 3, 0) + pltpu.roll(square, 2, 0) + pltpu.roll(square, 1, 0)
        if target:
            place, norm = -2.0 * place, norm + core_square
        whole = jnp.where(row == 3, norm, place)
        high = whole.astype(jnp.bfloat16).astype(jnp.float32)
        rest = whole - high
        middle = rest.astype(jnp.bfloat16).astype(jnp.float32)
        low = rest - middle
        upper = row < 4
        edge = (row == 3) | (row == 7)
        high_up, middle_up = pltpu.roll(high, 4, 0), pltpu.roll(middle, 4, 0)
        mixed = jnp.where(upper, high, middle_up)
        if target:
            low_up = pltpu.roll(low, 4, 0)
            parts = [
                mixed,
                jnp.where(row == 7, 1.0, jnp.where(upper, low, high_up)),
                jnp.where(edge, 1.0, mixed),
                jnp.where(edge, 0.0, jnp.where(upper, middle, low_up)),
            ]
        else:
            small = jnp.where(upper, low, middle_up)
            parts = [
                jnp.where(edge, 1.0, jnp.where(upper, high, high_up)),
                jnp.where(row == 3, 1.0, mixed),
                jnp.where(row == 7, high_up, small),
                small,
            ]
        return jnp.concatenate(parts, axis=0).astype(jnp.bfloat16)

    def prepare(i, block, target):
        if target:
            near[i] = features(block, True)
        far[i] = features(block, False).T
        terms[i] = products(block)

    def prepare_own(i, c):
        prepare(i, own[i], True)
        return c

    def ghost_copy(s, face):
        axis, low = face // 2, face % 2
        octants = ghost_out.at[s]
        bit = 1 - low
        part = (octants.at[bit], octants.at[:, bit], octants.at[:, :, bit])[axis]
        return remote(
            part,
            ghost_in.at[s, face],
            ghost_send.at[s, face],
            ghost_recv.at[s, face],
            neighbours[face],
        )

    def partner_copy(kind, s, axis):
        source, landing, send, recv, parts = kind
        span = pl.ds(0, parts * capacity)
        return remote(
            source.at[s, span],
            landing.at[s, axis, span],
            send.at[s, axis],
            recv.at[s, axis],
            partners[axis],
        )

    moved_inv = (inv_out, inv_in, inv_send, inv_recv, 6)
    moved_pos = (pos_out, pos_in, pos_send, pos_recv, 3)
    moved_vel = (vel_out, vel_in, vel_send, vel_recv, 3)

    def count_copy(axis):
        return remote(
            count_out, count_in.at[axis], count_send.at[axis], count_recv.at[axis], partners[axis]
        )

    def collect_arrivals(kind, got, s):
        landing, parts = kind[1], kind[4]
        cut = table[at["cut"] + s]
        first, second = cut == 0, cut == 1
        for k in range(parts * capacity // 8):
            span = pl.ds(8 * k, 8)
            later = jnp.where(second, landing[s, 1, span], landing[s, 2, span])
            got[span] = jnp.where(first, landing[s, 0, span], later)

    def limit_of(s):
        return jnp.minimum(table[at["count"] + s], counts[table[at["cut"] + s], s, 0, 0])

    def ghost_gather(s):
        for o in range(8):
            for q in range(4):
                pick = remap[table[at["ghost"] + o * 4 + q]]
                ghost_out[s, o // 4, (o // 2) % 2, o % 2, q] = own[pick]

    def weigh(t, out):
        product = jnp.dot(
            far[remap[table[at["source"] + t]]],
            near[remap[table[at["target"] + t]]],
            preferred_element_type=jnp.float32,
        )
        out[...] = (1.0 / jnp.maximum(product, core_square)).astype(jnp.bfloat16)

    def add_pair(t, weights, u, run):
        first = terms[remap[table[at["term"] + t]]]
        second = terms[remap[table[at["term"] + t + 1]]]
        left = jnp.concatenate([first, blank], axis=0)
        right = jnp.concatenate([blank, second], axis=0)
        both = jnp.dot(
            jnp.concatenate([left, right], axis=1).astype(jnp.bfloat16),
            jnp.concatenate([weights[u], weights[u + 1]], axis=0),
            preferred_element_type=jnp.float32,
        )
        for v in range(2):
            run = jnp.where(table[at["keep"] + t + v] != 0, run, 0.0) + both[8 * v : 8 * v + 8]
            sums[t + v] = run
        return run

    groups = tiles // GROUP

    def half(g, run, fill, ready):
        past = lax.rem(g + groups - 1, groups)
        for u in range(0, GROUP, 2):
            for v in range(2):
                weigh(g * GROUP + u + v, fill.at[u + v])
            run = add_pair(past * GROUP + u, ready, u, run)
        return run

    def two_groups(h, run):
        run = half(2 * h, run, weights_a, weights_b)
        return half(2 * h + 1, run, weights_b, weights_a)

    def collect(i, c):
        field[pl.ds(i, 8, stride=blocks), :] = sums[table[at["last"] + i]]
        return c

    def comp(ref, k):
        return ref[k * blocks : (k + 1) * blocks, :]

    def settle(s, pieces):
        limit = limit_of(s)

        def body(i, c):
            r = table[at["rank"] + s * blocks + i]
            spot = jnp.minimum(r, capacity - 1)
            for ref, base, got, parts in pieces:
                span = pl.ds(base * blocks + i, parts, stride=blocks)
                arrived = rows(got, spot, capacity, parts)
                ref[span, :] = jnp.where(r < limit, arrived, ref[span, :])
            return c

        lax.fori_loop(0, blocks, body, 0, unroll=8)

    placed = ((geo, 0, pos_got, 3), (inv, 0, inv_got, 6))

    def advance():
        scale = stress_coef / width
        sxx, syy, szz = (comp(field, k) * scale for k in (3, 4, 5))
        sxy, syz, sxz = (comp(field, k) * scale for k in (6, 7, 2))
        b = [comp(inv, k) for k in (3, 4, 5)]
        force = (
            sxx * b[0] + sxy * b[1] + sxz * b[2],
            sxy * b[0] + syy * b[1] + syz * b[2],
            sxz * b[0] + syz * b[1] + szz * b[2],
        )
        for k in range(3):
            velocity = comp(inv, k) * force[k]
            previous = comp(geo, 3 + k)
            geo[k * blocks : (k + 1) * blocks, :] = comp(geo, k) + time_step * (
                1.5 * velocity - 0.5 * previous
            )
            geo[(3 + k) * blocks : (4 + k) * blocks, :] = velocity
        geo[0 : 3 * blocks, :] = jnp.dot(
            geo[0 : 3 * blocks, :],
            matrix[...],
            precision=lax.Precision.HIGHEST,
            preferred_element_type=jnp.float32,
        )

    def gather_out(s, outs):
        def body(r, c):
            slot = table[at["mig"] + s * capacity + r]
            for ref, base, out, parts in outs:
                block = ref[pl.ds(base * blocks + slot, parts, stride=blocks), :]
                out[s, pl.ds(r, parts, stride=capacity), :] = block
            return c

        lax.fori_loop(0, capacity, body, 0, unroll=8)

    for axis in range(3):
        count_copy(axis).start()

    def step(s, carry):
        ghost_gather(s)
        for face in range(6):
            ghost_copy(s, face).start()

        @pl.when(s == 0)
        def _():
            lax.fori_loop(0, blocks, prepare_own, 0, unroll=8)
            for axis in range(3):
                count_copy(axis).wait_recv()
            local = pltpu.make_async_copy(count_in, counts, count_local)
            local.start()
            local.wait()

        @pl.when(s > 0)
        def _():
            settle(s - 1, placed)

            def prepare_arrived(r, c):
                prepare(blocks + r, own[blocks + r], True)
                return c

            lax.fori_loop(0, capacity, prepare_arrived, 0, unroll=8)

        gather_out(s, ((inv, 0, inv_out, 6),))
        for face in range(6):
            ghost_copy(s, face).wait_recv()

            def ghost_block(q, c, face=face):
                for u in range(4):
                    spot = held + face * 16 + q * 4 + u
                    prepare(spot, ghost_in[s, face, q // 2, q % 2, u], False)
                return c

            lax.fori_loop(0, 4, ghost_block, 0, unroll=2)
        for axis in range(3):
            partner_copy(moved_inv, s, axis).start()

        @pl.when(s > 0)
        def _():
            for axis in range(3):
                partner_copy(moved_vel, s - 1, axis).start()

        run = lax.fori_loop(0, groups // 2, two_groups, blank)
        for u in range(0, GROUP, 2):
            run = add_pair((groups - 1) * GROUP + u, weights_b, u, run)
        lax.fori_loop(0, blocks, collect, 0, unroll=8)

        @pl.when(s > 0)
        def _():
            for axis in range(3):
                partner_copy(moved_vel, s - 1, axis).wait_recv()
            collect_arrivals(moved_vel, vel_got, s - 1)
            settle(s - 1, ((geo, 3, vel_got, 3),))

        advance()
        gather_out(s, ((geo, 0, pos_out, 3), (geo, 3, vel_out, 3)))
        for axis in range(3):
            partner_copy(moved_pos, s, axis).start()

        @pl.when(s == STEPS - 1)
        def _():
            for axis in range(3):
                partner_copy(moved_vel, s, axis).start()

        @pl.when(s < STEPS - 1)
        def _():
            def rebuild(i, c):
                block = jnp.where(row < 3, rows(geo, i), rows(inv, i))
                own[i] = block
                prepare(i, block, True)
                return c

            lax.fori_loop(0, blocks, rebuild, 0, unroll=8)

        limit = limit_of(s)

        def route(i, c):
            r = table[at["rank"] + s * blocks + i]
            remap[i] = jnp.where(r < limit, blocks + r, i)
            return c

        lax.fori_loop(0, blocks, route, 0, unroll=8)
        for axis in range(3):
            partner_copy(moved_inv, s, axis).wait_recv()
        collect_arrivals(moved_inv, inv_got, s)
        for axis in range(3):
            partner_copy(moved_pos, s, axis).wait_recv()
        collect_arrivals(moved_pos, pos_got, s)

        @pl.when(s < STEPS - 1)
        def _():
            def arrive(r, c):
                place = rows(pos_got, r, capacity)
                own[blocks + r] = jnp.where(row < 3, place, rows(inv_got, r, capacity))
                return c

            lax.fori_loop(0, capacity, arrive, 0, unroll=8)

        for face in range(6):
            ghost_copy(s, face).wait_send()
        for axis in range(3):
            partner_copy(moved_inv, s, axis).wait_send()
            partner_copy(moved_pos, s, axis).wait_send()
        return carry

    lax.fori_loop(0, STEPS, step, 0)
    last = STEPS - 1
    settle(last, placed)
    for axis in range(3):
        partner_copy(moved_vel, last, axis).wait_recv()
    collect_arrivals(moved_vel, vel_got, last)
    settle(last, ((geo, 3, vel_got, 3),))

    def store_state(i, carry):
        g, v = rows(geo, i), rows(inv, i)
        result[i, 0:3, :] = g[0:3]
        result[i, 3:6, :] = v[3:6]
        result[i, 6:9, :] = g[3:6]
        result[i, 9:12, :] = v[0:3]
        return carry

    lax.fori_loop(0, blocks, store_state, 0, unroll=8)
    for axis in range(3):
        count_copy(axis).wait_send()
        for s in range(STEPS):
            partner_copy(moved_vel, s, axis).wait_send()


def on_device(
    segments, remesh_matrix, ghost_list, pair_list, tile_count, cut_axis, mig_list, mig_count
):
    blocks, _, width = segments.shape
    tiles = pair_list.shape[1]
    per_cell = ghost_list.shape[2]
    ghosts = 24 * per_cell
    capacity = mig_list.shape[2]
    at, _ = layout_of(tiles, blocks, 8 * per_cell, capacity)
    table = index_table(
        ghost_list, pair_list, tile_count, cut_axis, mig_list, mig_count, blocks, ghosts
    )
    vmem = pl.BlockSpec(memory_space=pltpu.VMEM)
    f32, bf16 = jnp.float32, jnp.bfloat16
    held = blocks + capacity
    return pl.pallas_call(
        functools.partial(kernel, at, (blocks, tiles, ghosts, capacity)),
        out_shape=jax.ShapeDtypeStruct(segments.shape, f32),
        in_specs=[pl.BlockSpec(memory_space=pltpu.SMEM), vmem, vmem],
        out_specs=vmem,
        scratch_shapes=[
            pltpu.VMEM((8 * blocks, width), f32),
            pltpu.VMEM((8 * blocks, width), f32),
            pltpu.VMEM((held, 8, width), f32),
            pltpu.VMEM((held, 32, width), bf16),
            pltpu.VMEM((held + ghosts, width, 32), bf16),
            pltpu.VMEM((held + ghosts + 1, 8, width), f32),
            pltpu.VMEM((GROUP, width, width), bf16),
            pltpu.VMEM((GROUP, width, width), bf16),
            pltpu.VMEM((tiles + 1, 8, width), f32),
            pltpu.VMEM((8 * blocks, width), f32),
            pltpu.SMEM((held + ghosts + 1,), jnp.int32),
            pltpu.SMEM((3, STEPS, 8, width), jnp.int32),
            pltpu.VMEM((STEPS, 8, width), jnp.int32),
            pltpu.VMEM((3, STEPS, 8, width), jnp.int32),
            pltpu.VMEM((STEPS, 2, 2, 2, per_cell, 8, width), f32),
            pltpu.VMEM((STEPS, 6, 2, 2, per_cell, 8, width), f32),
            pltpu.VMEM((STEPS, 8 * capacity, width), f32),
            pltpu.VMEM((STEPS, 3, 8 * capacity, width), f32),
            pltpu.VMEM((STEPS, 8 * capacity, width), f32),
            pltpu.VMEM((STEPS, 3, 8 * capacity, width), f32),
            pltpu.VMEM((STEPS, 8 * capacity, width), f32),
            pltpu.VMEM((STEPS, 3, 8 * capacity, width), f32),
            pltpu.VMEM((8 * capacity, width), f32),
            pltpu.VMEM((8 * capacity, width), f32),
            pltpu.VMEM((8 * capacity, width), f32),
            pltpu.SemaphoreType.DMA,
            pltpu.SemaphoreType.DMA((3,)),
            pltpu.SemaphoreType.DMA((3,)),
            pltpu.SemaphoreType.DMA((STEPS, 6)),
            pltpu.SemaphoreType.DMA((STEPS, 6)),
            pltpu.SemaphoreType.DMA((STEPS, 3)),
            pltpu.SemaphoreType.DMA((STEPS, 3)),
            pltpu.SemaphoreType.DMA((STEPS, 3)),
            pltpu.SemaphoreType.DMA((STEPS, 3)),
            pltpu.SemaphoreType.DMA((STEPS, 3)),
            pltpu.SemaphoreType.DMA((STEPS, 3)),
        ],
        compiler_params=pltpu.CompilerParams(
            collective_id=0, has_side_effects=True, vmem_limit_bytes=48 * 1024 * 1024
        ),
    )(table, segments, remesh_matrix)


def solution(mesh):
    return jax.shard_map(
        on_device,
        mesh=mesh,
        in_specs=(
            P(("gx", "gy", "gz"), None, None),
            P(),
            P(("gx", "gy", "gz"), None, None),
            P(("gx", "gy", "gz"), None, None),
            P(("gx", "gy", "gz")),
            P(),
            P(("gx", "gy", "gz"), None, None),
            P(("gx", "gy", "gz"), None),
        ),
        out_specs=P(("gx", "gy", "gz"), None, None),
        check_vma=False,
    )
```

time: 88.3 us -> 78.3 us (0.89)
  the two profiles are of different devices: /device:TPU:25 before, /device:TPU:5 now
where the time goes in v2:
time: 78.3 us; the launch traced here: 78.1 us
  Pallas kernels  71.6 us (91%)
  local copies, waits for them, and re-layouts  4.93 us (6%)
  other arithmetic  0.79 us (1%)
    pallas_call x1, Pallas kernels, on_device(): pl.pallas_call(functools.partial(kernel, at, (blocks, tiles, ghosts, capa...  71.6 us
    unnamed x15, local copies, waits for them, and re-layouts  3.72 us

profile of v2, /device:TPU:5, one launch (start us, length us, event | category | flops | bytes accessed | tf_op | source)
XLA Modules:
  0.0 78.1 jit_solution(4124285720055249015)
XLA Ops:
  0.7 0.0 copy-start.1
  0.7 0.7 copy-done.1
  1.3 0.1 select_reduce_fusion.1
  1.4 0.1 reshape.41
  1.5 0.0 copy-start.3
  1.5 0.1 reshape_squeeze.7
  1.6 0.6 copy-done.3
  2.2 0.0 copy-start.2
  2.2 0.1 copy.15
  2.3 0.1 reshape_squeeze.6
  2.4 0.5 copy-done.2
  2.9 0.1 convert_reduce_fusion.1
  3.1 0.2 convert_reduce_fusion
  3.3 0.2 select_reduce_fusion
  3.5 0.0 copy-start.4
  3.5 0.0 copy-start.5
  3.6 0.1 fusion.3
  3.6 0.6 copy-done.4
  4.2 0.0 copy-done.5
  4.2 0.1 concatenate.7.table
  4.3 0.0 copy-start
  4.3 1.3 %copy.16.segments = f32[64,12,128]{2,1,0:T(8,128)S(1)} copy(f32[64,12,128]{2,0,1:T(8,128)} %param.8) | data formatting | bytes 786432 | tf_op args[0]
  5.6 0.0 copy-done
  5.6 71.6 %shard_map.82 = f32[64,12,128]{2,1,0:T(8,128)S(1)} custom-call(s32[2414]{0:T(1024)S(1)} %concatenate.7.table, f32[64,12,128]{2,1,0:T(8,128)S(1)} %copy.16.segments, f32[128,128]{1,0:T(8,128)S(1)} %copy-done), custom_call_target="tpu_custom_call" | custom-call | tf_op jit(solution)/shard_map/pallas_call | solution.py:534
  77.2 0.9 %copy.17 = f32[64,12,128]{2,0,1:T(8,128)} copy(f32[64,12,128]{2,1,0:T(8,128)S(1)} %shard_map.82) | data formatting | bytes 786432 | tf_op jit(solution)/shard_map/pallas_call | solution.py:534
  (6 shorter events, 0.1 us)
Async XLA Ops:
  0.7 0.7 copy-start.1
  1.5 0.7 copy-start.3
  2.2 0.7 copy-start.2
  3.5 0.7 copy-start.4
  3.5 0.7 copy-start.5
  4.3 1.3 %copy-start = (f32[128,128]{1,0:T(8,128)S(1)}, f32[128,128]{1,0:T(8,128)}, u32[]{:S(2)}) copy-start(f32[128,128]{1,0:T(8,128)} %matrix.1) | copy-start | bytes 196612

commit v3 on v2

--- a/solution.py
+++ b/solution.py
@@ -14,7 +14,7 @@
 time_step = 0.5
 stress_coef = 0.25
 
-GROUP = 16
+GROUP = 32
 
 
 def layout_of(tiles, blocks, ghosts, slots):
@@ -87,7 +87,8 @@
     result,
     geo,
     inv,
-    own,
+    own_pos,
+    own_b,
     near,
     far,
     terms,
@@ -99,8 +100,10 @@
     counts,
     count_out,
     count_in,
-    ghost_out,
-    ghost_in,
+    gpos_out,
+    gpos_in,
+    gb_out,
+    gb_in,
     inv_out,
     inv_in,
     pos_out,
@@ -113,8 +116,10 @@
     count_local,
     count_send,
     count_recv,
-    ghost_send,
-    ghost_recv,
+    gpos_send,
+    gpos_recv,
+    gb_send,
+    gb_recv,
     inv_send,
     inv_recv,
     pos_send,
@@ -145,7 +150,10 @@
         pl.semaphore_signal(barrier, inc=1, device_id=device, device_id_type=MESH)
 
     row = lax.broadcasted_iota(jnp.int32, (8, width), 0)
+    upper = row < 4
+    edge = (row == 3) | (row == 7)
     blank = jnp.zeros((8, width), jnp.float32)
+    half_core = 0.5 * core_square
 
     def rows(ref, i, stride=blocks, count=8):
         return ref[pl.ds(i, count, stride=stride), :]
@@ -163,14 +171,19 @@
     def load_state(i, carry):
         block = segments[i]
         geo[pl.ds(i, 3, stride=blocks), :] = block[0:3]
-        geo[pl.ds(3 * blocks + i, 3, stride=blocks), :] = block[6:9]
-        inv[pl.ds(i, 3, stride=blocks), :] = block[9:12]
-        inv[pl.ds(3 * blocks + i, 3, stride=blocks), :] = block[3:6]
-        own[i] = block[0:8]
+        geo[pl.ds(4 * blocks + i, 3, stride=blocks), :] = block[6:9]
+        inv[pl.ds(i, 3, stride=blocks), :] = block[3:6]
+        inv[pl.ds(4 * blocks + i, 3, stride=blocks), :] = block[9:12]
+        place = block[0:8]
+        square = place * place
+        norm = pltpu.roll(square, 3, 0) + pltpu.roll(square, 2, 0) + pltpu.roll(square, 1, 0)
+        own_pos[i] = jnp.where(row < 3, place, norm + half_core)
+        own_b[i] = pltpu.roll(place, 5, 0)
         return carry
 
-    geo[6 * blocks : 8 * blocks, :] = jnp.zeros((2 * blocks, width), jnp.float32)
-    inv[6 * blocks : 8 * blocks, :] = jnp.zeros((2 * blocks, width), jnp.float32)
+    for ref in (geo, inv):
+        for k in (3, 7):
+            ref[k * blocks : (k + 1) * blocks, :] = jnp.zeros((blocks, width), jnp.float32)
     lax.fori_loop(0, blocks, load_state, 0, unroll=8)
     terms[held + ghosts] = blank
     sums[tiles] = blank
@@ -187,70 +200,72 @@
         count_out[s] = jnp.full((8, width), table[at["count"] + s], jnp.int32)
     pl.semaphore_wait(barrier, 9)
 
-    def products(block):
-        first = jnp.where(
-            row >= 6, pltpu.roll(block, 3, 0), jnp.where(row == 2, pltpu.roll(block, 7, 0), block)
-        )
-        second = jnp.where(
-            row >= 6, pltpu.roll(block, 2, 0), jnp.where(row == 2, pltpu.roll(block, 5, 0), block)
-        )
-        return first * second
-
-    def features(block, target):
-        place = jnp.where(row < 3, block, 0.0)
-        square = place * place
-        norm = pltpu.roll(square, 3, 0) + pltpu.roll(square, 2, 0) + pltpu.roll(square, 1, 0)
-        if target:
-            place, norm = -2.0 * place, norm + core_square
-        whole = jnp.where(row == 3, norm, place)
-        high = whole.astype(jnp.bfloat16).astype(jnp.float32)
-        rest = whole - high
+    def joined(first, second):
+        return jnp.where(upper, first, pltpu.roll(second, 4, 0))
+
+    def products(pair):
+        once, twice = pair * pltpu.roll(pair, 7, 0), pair * pltpu.roll(pair, 6, 0)
+        square = pair * pair
+        first = jnp.where(row == 3, pltpu.roll(twice, 3, 0), pltpu.roll(once, 4, 0))
+        second = jnp.where(row == 3, pltpu.roll(twice, 7, 0), once)
+        return (
+            jnp.where(row < 3, square, first),
+            jnp.where(row < 3, pltpu.roll(square, 4, 0), second),
+        )
+
+    def features(pair, i, target):
+        high = pair.astype(jnp.bfloat16).astype(jnp.float32)
+        rest = pair - high
         middle = rest.astype(jnp.bfloat16).astype(jnp.float32)
-        low = rest - middle
-        upper = row < 4
-        edge = (row == 3) | (row == 7)
-        high_up, middle_up = pltpu.roll(high, 4, 0), pltpu.roll(middle, 4, 0)
-        mixed = jnp.where(upper, high, middle_up)
-        if target:
-            low_up = pltpu.roll(low, 4, 0)
-            parts = [
-                mixed,
-                jnp.where(row == 7, 1.0, jnp.where(upper, low, high_up)),
-                jnp.where(edge, 1.0, mixed),
-                jnp.where(edge, 0.0, jnp.where(upper, middle, low_up)),
-            ]
-        else:
-            small = jnp.where(upper, low, middle_up)
-            parts = [
-                jnp.where(edge, 1.0, jnp.where(upper, high, high_up)),
+        parts = (high, middle, rest - middle)
+        turned = tuple(pltpu.roll(part, 4, 0) for part in parts)
+        factor = jnp.where(edge, 1.0, -2.0)
+        for v, (up, down) in enumerate(((parts, turned), (turned, parts))):
+            mixed = jnp.where(upper, up[0], down[1])
+            small = jnp.where(upper, up[2], down[1])
+            stack = [
+                jnp.where(edge, 1.0, jnp.where(upper, up[0], down[0])),
                 jnp.where(row == 3, 1.0, mixed),
-                jnp.where(row == 7, high_up, small),
+                jnp.where(row == 7, down[0], small),
                 small,
             ]
-        return jnp.concatenate(parts, axis=0).astype(jnp.bfloat16)
-
-    def prepare(i, block, target):
-        if target:
-            near[i] = features(block, True)
-        far[i] = features(block, False).T
-        terms[i] = products(block)
-
-    def prepare_own(i, c):
-        prepare(i, own[i], True)
+            far[i + v] = jnp.concatenate(stack, axis=0).astype(jnp.bfloat16).T
+            if target:
+                stack = [
+                    factor * mixed,
+                    jnp.where(row == 7, 1.0, factor * jnp.where(upper, up[2], down[0])),
+                    jnp.where(edge, 1.0, factor * mixed),
+                    jnp.where(edge, 0.0, factor * jnp.where(upper, up[1], down[2])),
+                ]
+                near[i + v] = jnp.concatenate(stack, axis=0).astype(jnp.bfloat16)
+
+    def prepare_own(h, c):
+        i = 2 * h
+        features(joined(own_pos[i], own_pos[i + 1]), i, True)
+        terms[i], terms[i + 1] = products(joined(own_b[i], own_b[i + 1]))
         return c
 
-    def ghost_copy(s, face):
+    def ghost_copy(kind, s, face):
+        source, landing, send, recv = kind
         axis, low = face // 2, face % 2
-        octants = ghost_out.at[s]
+        octants = source.at[s]
         bit = 1 - low
         part = (octants.at[bit], octants.at[:, bit], octants.at[:, :, bit])[axis]
         return remote(
-            part,
-            ghost_in.at[s, face],
-            ghost_send.at[s, face],
-            ghost_recv.at[s, face],
-            neighbours[face],
-        )
+            part, landing.at[s, face], send.at[s, face], recv.at[s, face], neighbours[face]
+        )
+
+    ghost_pos = (gpos_out, gpos_in, gpos_send, gpos_recv)
+    ghost_b = (gb_out, gb_in, gb_send, gb_recv)
+
+    def ghost_gather(kind, table_of, s):
+        for o in range(8):
+            for h in range(2):
+                base = at["ghost"] + o * 4 + 2 * h
+                first, second = table_of[remap[table[base]]], table_of[remap[table[base + 1]]]
+                kind[0][s, o // 4, (o // 2) % 2, o % 2, h] = joined(first, second)
+        for face in range(6):
+            ghost_copy(kind, s, face).start()
 
     def partner_copy(kind, s, axis):
         source, landing, send, recv, parts = kind
@@ -284,12 +299,6 @@
     def limit_of(s):
         return jnp.minimum(table[at["count"] + s], counts[table[at["cut"] + s], s, 0, 0])
 
-    def ghost_gather(s):
-        for o in range(8):
-            for q in range(4):
-                pick = remap[table[at["ghost"] + o * 4 + q]]
-                ghost_out[s, o // 4, (o // 2) % 2, o % 2, q] = own[pick]
-
     def weigh(t, out):
         product = jnp.dot(
             far[remap[table[at["source"] + t]]],
@@ -340,61 +349,65 @@
         def body(i, c):
             r = table[at["rank"] + s * blocks + i]
             spot = jnp.minimum(r, capacity - 1)
-            for ref, base, got, parts in pieces:
+            for ref, base, got, first, parts in pieces:
                 span = pl.ds(base * blocks + i, parts, stride=blocks)
-                arrived = rows(got, spot, capacity, parts)
+                arrived = rows(got, first * capacity + spot, capacity, parts)
                 ref[span, :] = jnp.where(r < limit, arrived, ref[span, :])
             return c
 
         lax.fori_loop(0, blocks, body, 0, unroll=8)
 
-    placed = ((geo, 0, pos_got, 3), (inv, 0, inv_got, 6))
+    placed = ((geo, 0, pos_got, 0, 3), (inv, 0, inv_got, 0, 3), (inv, 4, inv_got, 3, 3))
+
+    def norm_of(ref, count):
+        x, y, z = (ref[k * count : (k + 1) * count, :] for k in range(3))
+        return x * x + y * y + z * z + half_core
 
     def advance():
         scale = stress_coef / width
-        sxx, syy, szz = (comp(field, k) * scale for k in (3, 4, 5))
-        sxy, syz, sxz = (comp(field, k) * scale for k in (6, 7, 2))
-        b = [comp(inv, k) for k in (3, 4, 5)]
+        sxx, syy, szz = (comp(field, k) * scale for k in (0, 1, 2))
+        sxy, syz, sxz = (comp(field, k) * scale for k in (4, 5, 3))
+        b = [comp(inv, k) for k in (0, 1, 2)]
         force = (
             sxx * b[0] + sxy * b[1] + sxz * b[2],
             sxy * b[0] + syy * b[1] + syz * b[2],
             sxz * b[0] + syz * b[1] + szz * b[2],
         )
         for k in range(3):
-            velocity = comp(inv, k) * force[k]
-            previous = comp(geo, 3 + k)
+            velocity = comp(inv, 4 + k) * force[k]
+            previous = comp(geo, 4 + k)
             geo[k * blocks : (k + 1) * blocks, :] = comp(geo, k) + time_step * (
                 1.5 * velocity - 0.5 * previous
             )
-            geo[(3 + k) * blocks : (4 + k) * blocks, :] = velocity
+            geo[(4 + k) * blocks : (5 + k) * blocks, :] = velocity
         geo[0 : 3 * blocks, :] = jnp.dot(
             geo[0 : 3 * blocks, :],
             matrix[...],
             precision=lax.Precision.HIGHEST,
             preferred_element_type=jnp.float32,
         )
+        geo[3 * blocks : 4 * blocks, :] = norm_of(geo, blocks)
 
     def gather_out(s, outs):
         def body(r, c):
             slot = table[at["mig"] + s * capacity + r]
-            for ref, base, out, parts in outs:
+            for ref, base, out, first, parts in outs:
                 block = ref[pl.ds(base * blocks + slot, parts, stride=blocks), :]
-                out[s, pl.ds(r, parts, stride=capacity), :] = block
+                out[s, pl.ds(first * capacity + r, parts, stride=capacity), :] = block
             return c
 
         lax.fori_loop(0, capacity, body, 0, unroll=8)
 
     for axis in range(3):
         count_copy(axis).start()
+    ghost_gather(ghost_b, own_b, 0)
 
     def step(s, carry):
-        ghost_gather(s)
-        for face in range(6):
-            ghost_copy(s, face).start()
+        ghost_gather(ghost_pos, own_pos, s)
 
         @pl.when(s == 0)
         def _():
-            lax.fori_loop(0, blocks, prepare_own, 0, unroll=8)
+            lax.fori_loop(0, blocks // 2, prepare_own, 0, unroll=8)
             for axis in range(3):
                 count_copy(axis).wait_recv()
             local = pltpu.make_async_copy(count_in, counts, count_local)
@@ -403,25 +416,31 @@
 
         @pl.when(s > 0)
         def _():
+            lax.fori_loop(blocks // 2, held // 2, prepare_own, 0, unroll=6)
             settle(s - 1, placed)
 
-            def prepare_arrived(r, c):
-                prepare(blocks + r, own[blocks + r], True)
-                return c
-
-            lax.fori_loop(0, capacity, prepare_arrived, 0, unroll=8)
-
-        gather_out(s, ((inv, 0, inv_out, 6),))
+        gather_out(s, ((inv, 0, inv_out, 0, 3), (inv, 4, inv_out, 3, 3)))
         for face in range(6):
-            ghost_copy(s, face).wait_recv()
-
-            def ghost_block(q, c, face=face):
-                for u in range(4):
-                    spot = held + face * 16 + q * 4 + u
-                    prepare(spot, ghost_in[s, face, q // 2, q % 2, u], False)
-                return c
-
-            lax.fori_loop(0, 4, ghost_block, 0, unroll=2)
+            ghost_copy(ghost_b, s, face).wait_recv()
+
+        def ghost_terms(face, c):
+            for k in range(8):
+                spot = held + face * 16 + 2 * k
+                pair = gb_in[s, face, k // 4, (k // 2) % 2, k % 2]
+                terms[spot], terms[spot + 1] = products(pair)
+            return c
+
+        lax.fori_loop(0, 6, ghost_terms, 0, unroll=2)
+        for face in range(6):
+            ghost_copy(ghost_pos, s, face).wait_recv()
+
+        def ghost_features(face, c):
+            for k in range(8):
+                spot = held + face * 16 + 2 * k
+                features(gpos_in[s, face, k // 4, (k // 2) % 2, k % 2], spot, False)
+            return c
+
+        lax.fori_loop(0, 6, ghost_features, 0, unroll=2)
         for axis in range(3):
             partner_copy(moved_inv, s, axis).start()
 
@@ -440,54 +459,65 @@
             for axis in range(3):
                 partner_copy(moved_vel, s - 1, axis).wait_recv()
             collect_arrivals(moved_vel, vel_got, s - 1)
-            settle(s - 1, ((geo, 3, vel_got, 3),))
+            settle(s - 1, ((geo, 4, vel_got, 0, 3),))
 
         advance()
-        gather_out(s, ((geo, 0, pos_out, 3), (geo, 3, vel_out, 3)))
+        gather_out(s, ((geo, 0, pos_out, 0, 3),))
         for axis in range(3):
             partner_copy(moved_pos, s, axis).start()
+        gather_out(s, ((geo, 4, vel_out, 0, 3),))
 
         @pl.when(s == STEPS - 1)
         def _():
             for axis in range(3):
                 partner_copy(moved_vel, s, axis).start()
 
-        @pl.when(s < STEPS - 1)
-        def _():
-            def rebuild(i, c):
-                block = jnp.where(row < 3, rows(geo, i), rows(inv, i))
-                own[i] = block
-                prepare(i, block, True)
-                return c
-
-            lax.fori_loop(0, blocks, rebuild, 0, unroll=8)
-
-        limit = limit_of(s)
-
-        def route(i, c):
-            r = table[at["rank"] + s * blocks + i]
-            remap[i] = jnp.where(r < limit, blocks + r, i)
-            return c
-
-        lax.fori_loop(0, blocks, route, 0, unroll=8)
         for axis in range(3):
             partner_copy(moved_inv, s, axis).wait_recv()
         collect_arrivals(moved_inv, inv_got, s)
+
+        @pl.when(s < STEPS - 1)
+        def _():
+            limit = limit_of(s)
+
+            def route(i, c):
+                r = table[at["rank"] + s * blocks + i]
+                remap[i] = jnp.where(r < limit, blocks + r, i)
+                return c
+
+            lax.fori_loop(0, blocks, route, 0, unroll=8)
+
+            def arrive_b(r, c):
+                own_b[blocks + r] = rows(inv_got, r, capacity)
+                return c
+
+            def refresh(i, c):
+                own_pos[i] = rows(geo, i)
+                own_b[i] = rows(inv, i)
+                return c
+
+            lax.fori_loop(0, capacity, arrive_b, 0, unroll=8)
+            lax.fori_loop(0, blocks, refresh, 0, unroll=8)
+            ghost_gather(ghost_b, own_b, s + 1)
+            lax.fori_loop(0, blocks // 2, prepare_own, 0, unroll=8)
+
         for axis in range(3):
             partner_copy(moved_pos, s, axis).wait_recv()
         collect_arrivals(moved_pos, pos_got, s)
 
         @pl.when(s < STEPS - 1)
         def _():
+            pos_got[3 * capacity : 4 * capacity, :] = norm_of(pos_got, capacity)
+
             def arrive(r, c):
-                place = rows(pos_got, r, capacity)
-                own[blocks + r] = jnp.where(row < 3, place, rows(inv_got, r, capacity))
+                own_pos[blocks + r] = rows(pos_got, r, capacity)
                 return c
 
             lax.fori_loop(0, capacity, arrive, 0, unroll=8)
 
         for face in range(6):
-            ghost_copy(s, face).wait_send()
+            ghost_copy(ghost_b, s, face).wait_send()
+            ghost_copy(ghost_pos, s, face).wait_send()
         for axis in range(3):
             partner_copy(moved_inv, s, axis).wait_send()
             partner_copy(moved_pos, s, axis).wait_send()
@@ -499,14 +529,14 @@
     for axis in range(3):
         partner_copy(moved_vel, last, axis).wait_recv()
     collect_arrivals(moved_vel, vel_got, last)
-    settle(last, ((geo, 3, vel_got, 3),))
+    settle(last, ((geo, 4, vel_got, 0, 3),))
 
     def store_state(i, carry):
         g, v = rows(geo, i), rows(inv, i)
         result[i, 0:3, :] = g[0:3]
-        result[i, 3:6, :] = v[3:6]
-        result[i, 6:9, :] = g[3:6]
-        result[i, 9:12, :] = v[0:3]
+        result[i, 3:6, :] = v[0:3]
+        result[i, 6:9, :] = g[4:7]
+        result[i, 9:12, :] = v[4:7]
         return carry
 
     lax.fori_loop(0, blocks, store_state, 0, unroll=8)
@@ -540,6 +570,7 @@
             pltpu.VMEM((8 * blocks, width), f32),
             pltpu.VMEM((8 * blocks, width), f32),
             pltpu.VMEM((held, 8, width), f32),
+            pltpu.VMEM((held, 8, width), f32),
             pltpu.VMEM((held, 32, width), bf16),
             pltpu.VMEM((held + ghosts, width, 32), bf16),
             pltpu.VMEM((held + ghosts + 1, 8, width), f32),
@@ -551,8 +582,10 @@
             pltpu.SMEM((3, STEPS, 8, width), jnp.int32),
             pltpu.VMEM((STEPS, 8, width), jnp.int32),
             pltpu.VMEM((3, STEPS, 8, width), jnp.int32),
-            pltpu.VMEM((STEPS, 2, 2, 2, per_cell, 8, width), f32),
-            pltpu.VMEM((STEPS, 6, 2, 2, per_cell, 8, width), f32),
+            pltpu.VMEM((STEPS, 2, 2, 2, per_cell // 2, 8, width), f32),
+            pltpu.VMEM((STEPS, 6, 2, 2, per_cell // 2, 8, width), f32),
+            pltpu.VMEM((STEPS, 2, 2, 2, per_cell // 2, 8, width), f32),
+            pltpu.VMEM((STEPS, 6, 2, 2, per_cell // 2, 8, width), f32),
             pltpu.VMEM((STEPS, 8 * capacity, width), f32),
             pltpu.VMEM((STEPS, 3, 8 * capacity, width), f32),
             pltpu.VMEM((STEPS, 8 * capacity, width), f32),
@@ -565,6 +598,8 @@
             pltpu.SemaphoreType.DMA,
             pltpu.SemaphoreType.DMA((3,)),
             pltpu.SemaphoreType.DMA((3,)),
+            pltpu.SemaphoreType.DMA((STEPS, 6)),
+            pltpu.SemaphoreType.DMA((STEPS, 6)),
             pltpu.SemaphoreType.DMA((STEPS, 6)),
             pltpu.SemaphoreType.DMA((STEPS, 6)),
             pltpu.SemaphoreType.DMA((STEPS, 3)),

time: 78.3 us -> 74.5 us (0.951)
  the two profiles are of different devices: /device:TPU:5 before, /device:TPU:2 now
where the time goes in v3:
time: 74.5 us; the launch traced here: 73.8 us
  Pallas kernels  67.3 us (90%)
  local copies, waits for them, and re-layouts  4.93 us (7%)
  other arithmetic  0.79 us (1%)
    pallas_call x1, Pallas kernels, on_device(): pl.pallas_call(functools.partial(kernel, at, (blocks, tiles, ghosts, capa...  67.3 us
    unnamed x15, local copies, waits for them, and re-layouts  3.72 us

profile of v3, /device:TPU:2, one launch (start us, length us, event | category | flops | bytes accessed | tf_op | source)
XLA Modules:
  0.0 73.8 jit_solution(2935118733221795536)
XLA Ops:
  0.7 0.0 copy-start.1
  0.7 0.7 copy-done.1
  1.3 0.1 select_reduce_fusion.1
  1.4 0.1 reshape.41
  1.5 0.0 copy-start.3
  1.5 0.1 reshape_squeeze.7
  1.6 0.6 copy-done.3
  2.2 0.0 copy-start.2
  2.2 0.1 copy.15
  2.3 0.1 reshape_squeeze.6
  2.4 0.5 copy-done.2
  2.9 0.1 convert_reduce_fusion.1
  3.1 0.2 convert_reduce_fusion
  3.3 0.2 select_reduce_fusion
  3.5 0.0 copy-start.4
  3.5 0.0 copy-start.5
  3.6 0.1 fusion.3
  3.6 0.6 copy-done.4
  4.2 0.0 copy-done.5
  4.2 0.1 concatenate.7.table
  4.3 0.0 copy-start
  4.3 1.3 %copy.16.segments = f32[64,12,128]{2,1,0:T(8,128)S(1)} copy(f32[64,12,128]{2,0,1:T(8,128)} %param.8) | data formatting | bytes 786432 | tf_op args[0]
  5.6 0.0 copy-done
  5.6 67.3 %shard_map.82 = f32[64,12,128]{2,1,0:T(8,128)S(1)} custom-call(s32[2414]{0:T(1024)S(1)} %concatenate.7.table, f32[64,12,128]{2,1,0:T(8,128)S(1)} %copy.16.segments, f32[128,128]{1,0:T(8,128)S(1)} %copy-done), custom_call_target="tpu_custom_call" | custom-call | tf_op jit(solution)/shard_map/pallas_call | solution.py:564
  72.9 0.9 %copy.17 = f32[64,12,128]{2,0,1:T(8,128)} copy(f32[64,12,128]{2,1,0:T(8,128)S(1)} %shard_map.82) | data formatting | bytes 786432 | tf_op jit(solution)/shard_map/pallas_call | solution.py:564
  (6 shorter events, 0.1 us)
Async XLA Ops:
  0.7 0.7 copy-start.1
  1.5 0.7 copy-start.3
  2.2 0.7 copy-start.2
  3.5 0.7 copy-start.4
  3.5 0.7 copy-start.5
  4.3 1.3 %copy-start = (f32[128,128]{1,0:T(8,128)S(1)}, f32[128,128]{1,0:T(8,128)}, u32[]{:S(2)}) copy-start(f32[128,128]{1,0:T(8,128)} %matrix.1) | copy-start | bytes 196612

commit v4 on v3

--- a/solution.py
+++ b/solution.py
@@ -17,76 +17,25 @@
 GROUP = 32
 
 
-def layout_of(tiles, blocks, ghosts, slots):
-    sizes = dict(
-        target=tiles,
-        source=tiles,
-        term=tiles,
-        keep=tiles,
-        last=blocks,
-        ghost=ghosts,
-        mig=STEPS * slots,
-        rank=STEPS * blocks,
-        cut=STEPS,
-        count=STEPS,
-    )
-    offsets, total = {}, 0
-    for name, size in sizes.items():
-        offsets[name] = total
-        total += size
-    return offsets, total
-
-
-def index_table(ghost_list, pair_list, tile_count, cut_axis, mig_list, mig_count, blocks, ghosts):
-    tiles = pair_list.shape[1]
-    lists = mig_list[0]
-    capacity = lists.shape[1]
-    targets, origin = pair_list[0, :, 0], pair_list[0, :, 1]
-    number = jnp.arange(tiles, dtype=jnp.int32)
-    dead = (number >= tile_count[0]).astype(jnp.int32)
-    key = targets * tiles + number
-    place = jnp.sum((key[None, :] < key[:, None]).astype(jnp.int32), axis=1)
-    packed = (targets * 1024 + origin) * 2 + dead
-    hit = place[None, :] == number[:, None]
-    ordered = jnp.sum(jnp.where(hit, packed[None, :], 0), axis=1)
-    target = ordered // 2048
-    source = (ordered // 2) % 1024
-    source = jnp.where(source < blocks, source, source + capacity)
-    term = jnp.where(ordered % 2 == 1, blocks + capacity + ghosts, source)
-    before = jnp.concatenate([jnp.full((1,), -1, jnp.int32), target[:-1]])
-    keep = (target == before).astype(jnp.int32)
-    slot = jnp.arange(blocks, dtype=jnp.int32)
-    upto = jnp.sum((targets[None, :] <= slot[:, None]).astype(jnp.int32), axis=1)
-    own = jnp.sum((targets[None, :] == slot[:, None]).astype(jnp.int32), axis=1)
-    last = jnp.where(own > 0, upto - 1, tiles)
-    match = lists[:, None, :] == slot[None, :, None]
-    order = jnp.arange(capacity, dtype=jnp.int32)
-    rank = jnp.min(jnp.where(match, order[None, None, :], capacity), axis=2)
-    return jnp.concatenate(
-        [
-            target,
-            source,
-            term,
-            keep,
-            last,
-            ghost_list[0].reshape(-1),
-            lists.reshape(-1),
-            rank.reshape(-1),
-            cut_axis,
-            mig_count[0],
-        ]
-    )
+TARGET, SOURCE, TERM, KEEP, LAST, RANK = 0, 4, 8, 12, 16, 17
 
 
 def kernel(
-    at,
     sizes,
-    table,
+    pairs,
+    used,
+    ghost_list,
+    cuts,
+    lists,
+    amounts,
     segments,
-    matrix,
+    remesh,
     result,
     geo,
     inv,
+    matrix,
+    draft,
+    table,
     own_pos,
     own_b,
     near,
@@ -113,6 +62,7 @@
     inv_got,
     pos_got,
     vel_got,
+    load_sems,
     count_local,
     count_send,
     count_recv,
@@ -128,7 +78,7 @@
     vel_recv,
 ):
     blocks, tiles, ghosts, capacity = sizes
-    width = segments.shape[2]
+    width = segments.shape[1]
     held = blocks + capacity
     here = tuple(lax.axis_index(name) for name in ("gx", "gy", "gz"))
 
@@ -168,23 +118,22 @@
             device_id_type=MESH,
         )
 
-    def load_state(i, carry):
-        block = segments[i]
-        geo[pl.ds(i, 3, stride=blocks), :] = block[0:3]
-        geo[pl.ds(4 * blocks + i, 3, stride=blocks), :] = block[6:9]
-        inv[pl.ds(i, 3, stride=blocks), :] = block[3:6]
-        inv[pl.ds(4 * blocks + i, 3, stride=blocks), :] = block[9:12]
-        place = block[0:8]
-        square = place * place
-        norm = pltpu.roll(square, 3, 0) + pltpu.roll(square, 2, 0) + pltpu.roll(square, 1, 0)
-        own_pos[i] = jnp.where(row < 3, place, norm + half_core)
-        own_b[i] = pltpu.roll(place, 5, 0)
-        return carry
-
+    loads = (
+        (segments.at[pl.ds(0, 3 * blocks)], geo.at[pl.ds(0, 3 * blocks)]),
+        (segments.at[pl.ds(3 * blocks, 3 * blocks)], inv.at[pl.ds(0, 3 * blocks)]),
+        (segments.at[pl.ds(6 * blocks, 3 * blocks)], geo.at[pl.ds(4 * blocks, 3 * blocks)]),
+        (segments.at[pl.ds(9 * blocks, 3 * blocks)], inv.at[pl.ds(4 * blocks, 3 * blocks)]),
+        (remesh, matrix),
+    )
+    loads = [
+        pltpu.make_async_copy(source, landing, load_sems.at[k])
+        for k, (source, landing) in enumerate(loads)
+    ]
+    for load in loads:
+        load.start()
     for ref in (geo, inv):
         for k in (3, 7):
             ref[k * blocks : (k + 1) * blocks, :] = jnp.zeros((blocks, width), jnp.float32)
-    lax.fori_loop(0, blocks, load_state, 0, unroll=8)
     terms[held + ghosts] = blank
     sums[tiles] = blank
     weights_b[...] = jnp.zeros_like(weights_b)
@@ -195,10 +144,9 @@
         remap[i] = i
         return carry
 
-    lax.fori_loop(0, held + ghosts + 1, plain, 0)
+    lax.fori_loop(0, held + ghosts + 1, plain, 0, unroll=37)
     for s in range(STEPS):
-        count_out[s] = jnp.full((8, width), table[at["count"] + s], jnp.int32)
-    pl.semaphore_wait(barrier, 9)
+        count_out[s : s + 1, :] = jnp.full((1, width), amounts[0, s], jnp.int32)
 
     def joined(first, second):
         return jnp.where(upper, first, pltpu.roll(second, 4, 0))
@@ -258,14 +206,51 @@
     ghost_pos = (gpos_out, gpos_in, gpos_send, gpos_recv)
     ghost_b = (gb_out, gb_in, gb_send, gb_recv)
 
-    def ghost_gather(kind, table_of, s):
+    def ghost_gather(kind, block_of, s):
         for o in range(8):
             for h in range(2):
-                base = at["ghost"] + o * 4 + 2 * h
-                first, second = table_of[remap[table[base]]], table_of[remap[table[base + 1]]]
+                first = block_of(remap[ghost_list[2 * h, o]])
+                second = block_of(remap[ghost_list[2 * h + 1, o]])
                 kind[0][s, o // 4, (o // 2) % 2, o % 2, h] = joined(first, second)
         for face in range(6):
             ghost_copy(kind, s, face).start()
+
+    def note(line, values):
+        draft[pl.ds(line * width, width)] = values[0]
+
+    def order_pairs():
+        number = lax.broadcasted_iota(jnp.int32, (1, tiles), 1)
+        lane = lax.broadcasted_iota(jnp.int32, (1, width), 1)
+        key = pairs[0:1, :] * tiles + number
+        dead = jnp.where(number >= used[0], 1, 0)
+        packed = (pairs[0:1, :] * 1024 + pairs[1:2, :]) * 2 + dead
+        columns = jnp.concatenate([key, packed, jnp.zeros((6, tiles), jnp.int32)], axis=0).T
+        ordered = jnp.zeros((1, tiles), jnp.int32)
+        upto, before = jnp.zeros((1, width), jnp.int32), jnp.zeros((1, width), jnp.int32)
+        for c in range(0, tiles, width):
+            column = columns[c : c + width, 0:1]
+            place = jnp.sum(jnp.where(key < column, 1, 0), axis=1, keepdims=True)
+            content = columns[c : c + width, 1:2]
+            ordered += jnp.sum(jnp.where(place == number, content, 0), axis=0, keepdims=True)
+            upto += jnp.sum(
+                jnp.where(column < (lane + 1) * tiles, 1, 0), axis=0, keepdims=True
+            )
+            before += jnp.sum(jnp.where(column < lane * tiles, 1, 0), axis=0, keepdims=True)
+        source = lax.shift_right_logical(ordered, 1) & 1023
+        source = jnp.where(source < blocks, source, source + capacity)
+        target = lax.shift_right_logical(ordered, 11)
+        prior = pltpu.roll(jnp.broadcast_to(target, (8, tiles)), 1, 1)[0:1]
+        term = jnp.where((ordered & 1) == 1, held + ghosts, source)
+        keep = jnp.where((target == prior) & (number > 0), 1, 0)
+        for c in range(tiles // width):
+            for part, values in ((TARGET, target), (SOURCE, source), (TERM, term), (KEEP, keep)):
+                note(part + c, values[:, c * width : (c + 1) * width])
+        note(LAST, jnp.where(upto > before, upto - 1, tiles))
+        for s in range(STEPS):
+            rank = jnp.full((1, width), capacity, jnp.int32)
+            for r in range(capacity):
+                rank = jnp.where(lane == lists[s, 0, r], r, rank)
+            note(RANK + s, rank)
 
     def partner_copy(kind, s, axis):
         source, landing, send, recv, parts = kind
@@ -289,7 +274,7 @@
 
     def collect_arrivals(kind, got, s):
         landing, parts = kind[1], kind[4]
-        cut = table[at["cut"] + s]
+        cut = cuts[s]
         first, second = cut == 0, cut == 1
         for k in range(parts * capacity // 8):
             span = pl.ds(8 * k, 8)
@@ -297,19 +282,22 @@
             got[span] = jnp.where(first, landing[s, 0, span], later)
 
     def limit_of(s):
-        return jnp.minimum(table[at["count"] + s], counts[table[at["cut"] + s], s, 0, 0])
-
-    def weigh(t, out):
+        return jnp.minimum(amounts[0, s], counts[cuts[s], s, 0])
+
+    def entry(part, spot, u):
+        return table[spot + (part * width + u)]
+
+    def weigh(spot, u, out):
         product = jnp.dot(
-            far[remap[table[at["source"] + t]]],
-            near[remap[table[at["target"] + t]]],
+            far[remap[entry(SOURCE, spot, u)]],
+            near[remap[entry(TARGET, spot, u)]],
             preferred_element_type=jnp.float32,
         )
         out[...] = (1.0 / jnp.maximum(product, core_square)).astype(jnp.bfloat16)
 
-    def add_pair(t, weights, u, run):
-        first = terms[remap[table[at["term"] + t]]]
-        second = terms[remap[table[at["term"] + t + 1]]]
+    def add_pair(t, spot, weights, u, run):
+        first = terms[remap[entry(TERM, spot, u)]]
+        second = terms[remap[entry(TERM, spot, u + 1)]]
         left = jnp.concatenate([first, blank], axis=0)
         right = jnp.concatenate([blank, second], axis=0)
         both = jnp.dot(
@@ -318,18 +306,22 @@
             preferred_element_type=jnp.float32,
         )
         for v in range(2):
-            run = jnp.where(table[at["keep"] + t + v] != 0, run, 0.0) + both[8 * v : 8 * v + 8]
-            sums[t + v] = run
+            run = jnp.where(entry(KEEP, spot, u + v) != 0, run, 0.0) + both[8 * v : 8 * v + 8]
+            sums[t + u + v] = run
         return run
+
+    def spot_of(g):
+        return g * GROUP
 
     groups = tiles // GROUP
 
     def half(g, run, fill, ready):
         past = lax.rem(g + groups - 1, groups)
+        spot, before = spot_of(g), spot_of(past)
         for u in range(0, GROUP, 2):
             for v in range(2):
-                weigh(g * GROUP + u + v, fill.at[u + v])
-            run = add_pair(past * GROUP + u, ready, u, run)
+                weigh(spot, u + v, fill.at[u + v])
+            run = add_pair(past * GROUP, before, ready, u, run)
         return run
 
     def two_groups(h, run):
@@ -337,7 +329,7 @@
         return half(2 * h + 1, run, weights_b, weights_a)
 
     def collect(i, c):
-        field[pl.ds(i, 8, stride=blocks), :] = sums[table[at["last"] + i]]
+        field[pl.ds(i, 8, stride=blocks), :] = sums[table[LAST * width + i]]
         return c
 
     def comp(ref, k):
@@ -347,12 +339,17 @@
         limit = limit_of(s)
 
         def body(i, c):
-            r = table[at["rank"] + s * blocks + i]
+            r = table[(RANK + s) * width + i]
             spot = jnp.minimum(r, capacity - 1)
-            for ref, base, got, first, parts in pieces:
+            for ref, base, got, first, parts, *target in pieces:
                 span = pl.ds(base * blocks + i, parts, stride=blocks)
                 arrived = rows(got, first * capacity + spot, capacity, parts)
-                ref[span, :] = jnp.where(r < limit, arrived, ref[span, :])
+                fresh = jnp.where(r < limit, arrived, ref[span, :])
+                if target:
+                    out, at = target
+                    out[pl.ds(at * blocks + i, parts, stride=blocks), :] = fresh
+                else:
+                    ref[span, :] = fresh
             return c
 
         lax.fori_loop(0, blocks, body, 0, unroll=8)
@@ -390,7 +387,7 @@
 
     def gather_out(s, outs):
         def body(r, c):
-            slot = table[at["mig"] + s * capacity + r]
+            slot = lists[s, 0, r]
             for ref, base, out, first, parts in outs:
                 block = ref[pl.ds(base * blocks + slot, parts, stride=blocks), :]
                 out[s, pl.ds(first * capacity + r, parts, stride=capacity), :] = block
@@ -398,22 +395,35 @@
 
         lax.fori_loop(0, capacity, body, 0, unroll=8)
 
+    for load in loads[:4]:
+        load.wait()
+    geo[3 * blocks : 4 * blocks, :] = norm_of(geo, blocks)
+    pl.semaphore_wait(barrier, 9)
+    ghost_gather(ghost_pos, lambda pick: rows(geo, pick), 0)
+    ghost_gather(ghost_b, lambda pick: rows(inv, pick), 0)
     for axis in range(3):
         count_copy(axis).start()
-    ghost_gather(ghost_b, own_b, 0)
+    order_pairs()
+    ordering = pltpu.make_async_copy(draft, table, load_sems.at[5])
+    ordering.start()
+    for load in loads[4:]:
+        load.wait()
+
+    def refresh(i, c):
+        own_pos[i] = rows(geo, i)
+        own_b[i] = rows(inv, i)
+        return c
+
+    lax.fori_loop(0, blocks, refresh, 0, unroll=8)
+    lax.fori_loop(0, blocks // 2, prepare_own, 0, unroll=8)
+    for axis in range(3):
+        count_copy(axis).wait_recv()
+    local = pltpu.make_async_copy(count_in, counts, count_local)
+    local.start()
+    local.wait()
+    ordering.wait()
 
     def step(s, carry):
-        ghost_gather(ghost_pos, own_pos, s)
-
-        @pl.when(s == 0)
-        def _():
-            lax.fori_loop(0, blocks // 2, prepare_own, 0, unroll=8)
-            for axis in range(3):
-                count_copy(axis).wait_recv()
-            local = pltpu.make_async_copy(count_in, counts, count_local)
-            local.start()
-            local.wait()
-
         @pl.when(s > 0)
         def _():
             lax.fori_loop(blocks // 2, held // 2, prepare_own, 0, unroll=6)
@@ -451,7 +461,7 @@
 
         run = lax.fori_loop(0, groups // 2, two_groups, blank)
         for u in range(0, GROUP, 2):
-            run = add_pair((groups - 1) * GROUP + u, weights_b, u, run)
+            run = add_pair((groups - 1) * GROUP, spot_of(jnp.int32(groups - 1)), weights_b, u, run)
         lax.fori_loop(0, blocks, collect, 0, unroll=8)
 
         @pl.when(s > 0)
@@ -481,7 +491,7 @@
             limit = limit_of(s)
 
             def route(i, c):
-                r = table[at["rank"] + s * blocks + i]
+                r = table[(RANK + s) * width + i]
                 remap[i] = jnp.where(r < limit, blocks + r, i)
                 return c
 
@@ -491,15 +501,15 @@
                 own_b[blocks + r] = rows(inv_got, r, capacity)
                 return c
 
-            def refresh(i, c):
-                own_pos[i] = rows(geo, i)
-                own_b[i] = rows(inv, i)
-                return c
-
             lax.fori_loop(0, capacity, arrive_b, 0, unroll=8)
             lax.fori_loop(0, blocks, refresh, 0, unroll=8)
-            ghost_gather(ghost_b, own_b, s + 1)
+            ghost_gather(ghost_b, lambda pick: own_b[pick], s + 1)
             lax.fori_loop(0, blocks // 2, prepare_own, 0, unroll=8)
+
+        @pl.when(s == STEPS - 1)
+        def _():
+            final = ((inv, 0, inv_got, 0, 3, result, 3), (inv, 4, inv_got, 3, 3, result, 9))
+            settle(s, final)
 
         for axis in range(3):
             partner_copy(moved_pos, s, axis).wait_recv()
@@ -514,6 +524,7 @@
                 return c
 
             lax.fori_loop(0, capacity, arrive, 0, unroll=8)
+            ghost_gather(ghost_pos, lambda pick: own_pos[pick], s + 1)
 
         for face in range(6):
             ghost_copy(ghost_b, s, face).wait_send()
@@ -525,21 +536,11 @@
 
     lax.fori_loop(0, STEPS, step, 0)
     last = STEPS - 1
-    settle(last, placed)
+    settle(last, ((geo, 0, pos_got, 0, 3, result, 0),))
     for axis in range(3):
         partner_copy(moved_vel, last, axis).wait_recv()
     collect_arrivals(moved_vel, vel_got, last)
-    settle(last, ((geo, 4, vel_got, 0, 3),))
-
-    def store_state(i, carry):
-        g, v = rows(geo, i), rows(inv, i)
-        result[i, 0:3, :] = g[0:3]
-        result[i, 3:6, :] = v[0:3]
-        result[i, 6:9, :] = g[4:7]
-        result[i, 9:12, :] = v[4:7]
-        return carry
-
-    lax.fori_loop(0, blocks, store_state, 0, unroll=8)
+    settle(last, ((geo, 4, vel_got, 0, 3, result, 6),))
     for axis in range(3):
         count_copy(axis).wait_send()
         for s in range(STEPS):
@@ -554,21 +555,20 @@
     per_cell = ghost_list.shape[2]
     ghosts = 24 * per_cell
     capacity = mig_list.shape[2]
-    at, _ = layout_of(tiles, blocks, 8 * per_cell, capacity)
-    table = index_table(
-        ghost_list, pair_list, tile_count, cut_axis, mig_list, mig_count, blocks, ghosts
-    )
-    vmem = pl.BlockSpec(memory_space=pltpu.VMEM)
+    vmem, smem = (pl.BlockSpec(memory_space=m) for m in (pltpu.VMEM, pltpu.SMEM))
     f32, bf16 = jnp.float32, jnp.bfloat16
     held = blocks + capacity
-    return pl.pallas_call(
-        functools.partial(kernel, at, (blocks, tiles, ghosts, capacity)),
-        out_shape=jax.ShapeDtypeStruct(segments.shape, f32),
-        in_specs=[pl.BlockSpec(memory_space=pltpu.SMEM), vmem, vmem],
+    result = pl.pallas_call(
+        functools.partial(kernel, (blocks, tiles, ghosts, capacity)),
+        out_shape=jax.ShapeDtypeStruct((12 * blocks, width), f32),
+        in_specs=[vmem] + [smem] * 5 + [pl.BlockSpec(memory_space=pltpu.HBM)] * 2,
         out_specs=vmem,
         scratch_shapes=[
             pltpu.VMEM((8 * blocks, width), f32),
             pltpu.VMEM((8 * blocks, width), f32),
+            pltpu.VMEM((width, width), f32),
+            pltpu.VMEM((24 * width,), jnp.int32),
+            pltpu.SMEM((24 * width,), jnp.int32),
             pltpu.VMEM((held, 8, width), f32),
             pltpu.VMEM((held, 8, width), f32),
             pltpu.VMEM((held, 32, width), bf16),
@@ -579,9 +579,9 @@
             pltpu.VMEM((tiles + 1, 8, width), f32),
             pltpu.VMEM((8 * blocks, width), f32),
             pltpu.SMEM((held + ghosts + 1,), jnp.int32),
-            pltpu.SMEM((3, STEPS, 8, width), jnp.int32),
-            pltpu.VMEM((STEPS, 8, width), jnp.int32),
-            pltpu.VMEM((3, STEPS, 8, width), jnp.int32),
+            pltpu.SMEM((3, 8, width), jnp.int32),
+            pltpu.VMEM((8, width), jnp.int32),
+            pltpu.VMEM((3, 8, width), jnp.int32),
             pltpu.VMEM((STEPS, 2, 2, 2, per_cell // 2, 8, width), f32),
             pltpu.VMEM((STEPS, 6, 2, 2, per_cell // 2, 8, width), f32),
             pltpu.VMEM((STEPS, 2, 2, 2, per_cell // 2, 8, width), f32),
@@ -595,6 +595,7 @@
             pltpu.VMEM((8 * capacity, width), f32),
             pltpu.VMEM((8 * capacity, width), f32),
             pltpu.VMEM((8 * capacity, width), f32),
+            pltpu.SemaphoreType.DMA((6,)),
             pltpu.SemaphoreType.DMA,
             pltpu.SemaphoreType.DMA((3,)),
             pltpu.SemaphoreType.DMA((3,)),
@@ -610,9 +611,19 @@
             pltpu.SemaphoreType.DMA((STEPS, 3)),
         ],
         compiler_params=pltpu.CompilerParams(
-            collective_id=0, has_side_effects=True, vmem_limit_bytes=48 * 1024 * 1024
+            collective_id=0, has_side_effects=True, vmem_limit_bytes=63 * 1024 * 1024
         ),
-    )(table, segments, remesh_matrix)
+    )(
+        pair_list[0].T,
+        tile_count,
+        ghost_list[0].T,
+        cut_axis,
+        jnp.transpose(mig_list, (1, 0, 2)),
+        mig_count,
+        jnp.transpose(segments, (1, 0, 2)).reshape(12 * blocks, width),
+        remesh_matrix,
+    )
+    return jnp.transpose(result.reshape(12, blocks, width), (1, 0, 2))
 
 
 def solution(mesh):

time: 74.5 us -> 71.9 us (0.965)
  local copies, waits for them, and re-layouts: 4.93 us -> 1.77 us
  Pallas kernels: 67.3 us -> 69.1 us
  other arithmetic: 0.79 us -> 0 us
    unnamed x15 -> x1, local copies, waits for them, and re-layouts: 3.72 us -> 1.77 us
    pallas_call x1, Pallas kernels: 67.3 us -> 69.1 us  [on_device(): pl.pallas_call(functools.partial(kernel, (blocks, tiles, ghosts, capacity...]
    pallas_call x1 -> x0, local copies, waits for them, and re-layouts: 0.87 us -> none  [on_device(): pl.pallas_call(functools.partial(kernel, at, (blocks, tiles, ghosts, capa...]
where the time goes in v4:
time: 71.9 us; the launch traced here: 71.6 us
  Pallas kernels  69.1 us (96%)
  local copies, waits for them, and re-layouts  1.77 us (2%)
    pallas_call x1, Pallas kernels, on_device(): pl.pallas_call(functools.partial(kernel, (blocks, tiles, ghosts, capacity...  69.1 us
    unnamed x1, local copies, waits for them, and re-layouts  1.77 us

profile of v4, /device:TPU:2, one launch (start us, length us, event | category | flops | bytes accessed | tf_op | source)
XLA Modules:
  0.0 71.6 jit_solution(15704056578584279857)
XLA Ops:
  0.7 69.1 %shard_map.82 = f32[768,128]{1,0:T(8,128)} custom-call(s32[2,512]{1,0:T(2,128)} %bitcast.15, s32[1]{0:T(128)S(6)} %copy.10.used, s32[4,8]{1,0:T(4,128)} %bitcast.16, s32[3]{0:T(128)} %cuts.1, s32[3,1,24]{2,1,0:T(1,128)} %bitcast.17, s32[1,3]{1,0:T(1,128)} %amounts.1, f32[768,128]{1,0:T(8,128)} %bitcast.14, f32[128,128]{1,0:T(8,128)} %remesh.1), custom_call_target="tpu_custom_call" | custom-call | tf_op jit(solution)/shard_map/pallas_call | solution.py:561
  69.8 1.8 %copy.11 = f32[64,12,128]{2,0,1:T(8,128)} copy(f32[64,12,128]{2,0,1:T(8,128)} %bitcast.13) | data formatting | bytes 786432

commit v5 on v4

--- a/solution.py
+++ b/solution.py
@@ -22,10 +22,10 @@
 
 def kernel(
     sizes,
+    cut_order,
     pairs,
     used,
     ghost_list,
-    cuts,
     lists,
     amounts,
     segments,
@@ -95,6 +95,15 @@
         shifted(axis, lax.axis_size(name) // 2) for axis, name in enumerate(("gx", "gy", "gz"))
     ]
 
+    def partner_of(s):
+        place = []
+        for axis, name in enumerate(("gx", "gy", "gz")):
+            apart = s - cut_order.index(axis)
+            here_cut = 1 - (apart * apart + 3) // 4
+            count = lax.axis_size(name)
+            place.append(lax.rem(here[axis] + here_cut * (count // 2), count))
+        return tuple(place)
+
     barrier = pltpu.get_barrier_semaphore()
     for device in neighbours + partners:
         pl.semaphore_signal(barrier, inc=1, device_id=device, device_id_type=MESH)
@@ -252,37 +261,28 @@
                 rank = jnp.where(lane == lists[s, 0, r], r, rank)
             note(RANK + s, rank)
 
-    def partner_copy(kind, s, axis):
+    def partner_copy(kind, s):
         source, landing, send, recv, parts = kind
         span = pl.ds(0, parts * capacity)
         return remote(
-            source.at[s, span],
-            landing.at[s, axis, span],
-            send.at[s, axis],
-            recv.at[s, axis],
-            partners[axis],
+            source.at[s, span], landing.at[s, span], send.at[s], recv.at[s], partner_of(s)
         )
 
     moved_inv = (inv_out, inv_in, inv_send, inv_recv, 6)
     moved_pos = (pos_out, pos_in, pos_send, pos_recv, 3)
     moved_vel = (vel_out, vel_in, vel_send, vel_recv, 3)
 
-    def count_copy(axis):
-        return remote(
-            count_out, count_in.at[axis], count_send.at[axis], count_recv.at[axis], partners[axis]
-        )
+    def count_copy(s):
+        return remote(count_out, count_in.at[s], count_send.at[s], count_recv.at[s], partner_of(s))
 
     def collect_arrivals(kind, got, s):
         landing, parts = kind[1], kind[4]
-        cut = cuts[s]
-        first, second = cut == 0, cut == 1
         for k in range(parts * capacity // 8):
             span = pl.ds(8 * k, 8)
-            later = jnp.where(second, landing[s, 1, span], landing[s, 2, span])
-            got[span] = jnp.where(first, landing[s, 0, span], later)
+            got[span] = landing[s, span]
 
     def limit_of(s):
-        return jnp.minimum(amounts[0, s], counts[cuts[s], s, 0])
+        return jnp.minimum(amounts[0, s], counts[s, s, 0])
 
     def entry(part, spot, u):
         return table[spot + (part * width + u)]
@@ -395,17 +395,17 @@
 
         lax.fori_loop(0, capacity, body, 0, unroll=8)
 
+    order_pairs()
+    ordering = pltpu.make_async_copy(draft, table, load_sems.at[5])
+    ordering.start()
     for load in loads[:4]:
         load.wait()
     geo[3 * blocks : 4 * blocks, :] = norm_of(geo, blocks)
     pl.semaphore_wait(barrier, 9)
     ghost_gather(ghost_pos, lambda pick: rows(geo, pick), 0)
     ghost_gather(ghost_b, lambda pick: rows(inv, pick), 0)
-    for axis in range(3):
-        count_copy(axis).start()
-    order_pairs()
-    ordering = pltpu.make_async_copy(draft, table, load_sems.at[5])
-    ordering.start()
+    for s in range(STEPS):
+        count_copy(s).start()
     for load in loads[4:]:
         load.wait()
 
@@ -416,8 +416,8 @@
 
     lax.fori_loop(0, blocks, refresh, 0, unroll=8)
     lax.fori_loop(0, blocks // 2, prepare_own, 0, unroll=8)
-    for axis in range(3):
-        count_copy(axis).wait_recv()
+    for s in range(STEPS):
+        count_copy(s).wait_recv()
     local = pltpu.make_async_copy(count_in, counts, count_local)
     local.start()
     local.wait()
@@ -451,13 +451,11 @@
             return c
 
         lax.fori_loop(0, 6, ghost_features, 0, unroll=2)
-        for axis in range(3):
-            partner_copy(moved_inv, s, axis).start()
+        partner_copy(moved_inv, s).start()
 
         @pl.when(s > 0)
         def _():
-            for axis in range(3):
-                partner_copy(moved_vel, s - 1, axis).start()
+            partner_copy(moved_vel, s - 1).start()
 
         run = lax.fori_loop(0, groups // 2, two_groups, blank)
         for u in range(0, GROUP, 2):
@@ -466,24 +464,20 @@
 
         @pl.when(s > 0)
         def _():
-            for axis in range(3):
-                partner_copy(moved_vel, s - 1, axis).wait_recv()
+            partner_copy(moved_vel, s - 1).wait_recv()
             collect_arrivals(moved_vel, vel_got, s - 1)
             settle(s - 1, ((geo, 4, vel_got, 0, 3),))
 
         advance()
         gather_out(s, ((geo, 0, pos_out, 0, 3),))
-        for axis in range(3):
-            partner_copy(moved_pos, s, axis).start()
+        partner_copy(moved_pos, s).start()
         gather_out(s, ((geo, 4, vel_out, 0, 3),))
 
         @pl.when(s == STEPS - 1)
         def _():
-            for axis in range(3):
-                partner_copy(moved_vel, s, axis).start()
-
-        for axis in range(3):
-            partner_copy(moved_inv, s, axis).wait_recv()
+            partner_copy(moved_vel, s).start()
+
+        partner_copy(moved_inv, s).wait_recv()
         collect_arrivals(moved_inv, inv_got, s)
 
         @pl.when(s < STEPS - 1)
@@ -511,8 +505,7 @@
             final = ((inv, 0, inv_got, 0, 3, result, 3), (inv, 4, inv_got, 3, 3, result, 9))
             settle(s, final)
 
-        for axis in range(3):
-            partner_copy(moved_pos, s, axis).wait_recv()
+        partner_copy(moved_pos, s).wait_recv()
         collect_arrivals(moved_pos, pos_got, s)
 
         @pl.when(s < STEPS - 1)
@@ -529,22 +522,19 @@
         for face in range(6):
             ghost_copy(ghost_b, s, face).wait_send()
             ghost_copy(ghost_pos, s, face).wait_send()
-        for axis in range(3):
-            partner_copy(moved_inv, s, axis).wait_send()
-            partner_copy(moved_pos, s, axis).wait_send()
+        partner_copy(moved_inv, s).wait_send()
+        partner_copy(moved_pos, s).wait_send()
         return carry
 
     lax.fori_loop(0, STEPS, step, 0)
     last = STEPS - 1
     settle(last, ((geo, 0, pos_got, 0, 3, result, 0),))
-    for axis in range(3):
-        partner_copy(moved_vel, last, axis).wait_recv()
+    partner_copy(moved_vel, last).wait_recv()
     collect_arrivals(moved_vel, vel_got, last)
     settle(last, ((geo, 4, vel_got, 0, 3, result, 6),))
-    for axis in range(3):
-        count_copy(axis).wait_send()
-        for s in range(STEPS):
-            partner_copy(moved_vel, s, axis).wait_send()
+    for s in range(STEPS):
+        count_copy(s).wait_send()
+        partner_copy(moved_vel, s).wait_send()
 
 
 def on_device(
@@ -558,66 +548,75 @@
     vmem, smem = (pl.BlockSpec(memory_space=m) for m in (pltpu.VMEM, pltpu.SMEM))
     f32, bf16 = jnp.float32, jnp.bfloat16
     held = blocks + capacity
-    result = pl.pallas_call(
-        functools.partial(kernel, (blocks, tiles, ghosts, capacity)),
-        out_shape=jax.ShapeDtypeStruct((12 * blocks, width), f32),
-        in_specs=[vmem] + [smem] * 5 + [pl.BlockSpec(memory_space=pltpu.HBM)] * 2,
-        out_specs=vmem,
-        scratch_shapes=[
-            pltpu.VMEM((8 * blocks, width), f32),
-            pltpu.VMEM((8 * blocks, width), f32),
-            pltpu.VMEM((width, width), f32),
-            pltpu.VMEM((24 * width,), jnp.int32),
-            pltpu.SMEM((24 * width,), jnp.int32),
-            pltpu.VMEM((held, 8, width), f32),
-            pltpu.VMEM((held, 8, width), f32),
-            pltpu.VMEM((held, 32, width), bf16),
-            pltpu.VMEM((held + ghosts, width, 32), bf16),
-            pltpu.VMEM((held + ghosts + 1, 8, width), f32),
-            pltpu.VMEM((GROUP, width, width), bf16),
-            pltpu.VMEM((GROUP, width, width), bf16),
-            pltpu.VMEM((tiles + 1, 8, width), f32),
-            pltpu.VMEM((8 * blocks, width), f32),
-            pltpu.SMEM((held + ghosts + 1,), jnp.int32),
-            pltpu.SMEM((3, 8, width), jnp.int32),
-            pltpu.VMEM((8, width), jnp.int32),
-            pltpu.VMEM((3, 8, width), jnp.int32),
-            pltpu.VMEM((STEPS, 2, 2, 2, per_cell // 2, 8, width), f32),
-            pltpu.VMEM((STEPS, 6, 2, 2, per_cell // 2, 8, width), f32),
-            pltpu.VMEM((STEPS, 2, 2, 2, per_cell // 2, 8, width), f32),
-            pltpu.VMEM((STEPS, 6, 2, 2, per_cell // 2, 8, width), f32),
-            pltpu.VMEM((STEPS, 8 * capacity, width), f32),
-            pltpu.VMEM((STEPS, 3, 8 * capacity, width), f32),
-            pltpu.VMEM((STEPS, 8 * capacity, width), f32),
-            pltpu.VMEM((STEPS, 3, 8 * capacity, width), f32),
-            pltpu.VMEM((STEPS, 8 * capacity, width), f32),
-            pltpu.VMEM((STEPS, 3, 8 * capacity, width), f32),
-            pltpu.VMEM((8 * capacity, width), f32),
-            pltpu.VMEM((8 * capacity, width), f32),
-            pltpu.VMEM((8 * capacity, width), f32),
-            pltpu.SemaphoreType.DMA((6,)),
-            pltpu.SemaphoreType.DMA,
-            pltpu.SemaphoreType.DMA((3,)),
-            pltpu.SemaphoreType.DMA((3,)),
-            pltpu.SemaphoreType.DMA((STEPS, 6)),
-            pltpu.SemaphoreType.DMA((STEPS, 6)),
-            pltpu.SemaphoreType.DMA((STEPS, 6)),
-            pltpu.SemaphoreType.DMA((STEPS, 6)),
-            pltpu.SemaphoreType.DMA((STEPS, 3)),
-            pltpu.SemaphoreType.DMA((STEPS, 3)),
-            pltpu.SemaphoreType.DMA((STEPS, 3)),
-            pltpu.SemaphoreType.DMA((STEPS, 3)),
-            pltpu.SemaphoreType.DMA((STEPS, 3)),
-            pltpu.SemaphoreType.DMA((STEPS, 3)),
-        ],
-        compiler_params=pltpu.CompilerParams(
-            collective_id=0, has_side_effects=True, vmem_limit_bytes=63 * 1024 * 1024
-        ),
-    )(
+    scratch = [
+        pltpu.VMEM((8 * blocks, width), f32),
+        pltpu.VMEM((8 * blocks, width), f32),
+        pltpu.VMEM((width, width), f32),
+        pltpu.VMEM((24 * width,), jnp.int32),
+        pltpu.SMEM((24 * width,), jnp.int32),
+        pltpu.VMEM((held, 8, width), f32),
+        pltpu.VMEM((held, 8, width), f32),
+        pltpu.VMEM((held, 32, width), bf16),
+        pltpu.VMEM((held + ghosts, width, 32), bf16),
+        pltpu.VMEM((held + ghosts + 1, 8, width), f32),
+        pltpu.VMEM((GROUP, width, width), bf16),
+        pltpu.VMEM((GROUP, width, width), bf16),
+        pltpu.VMEM((tiles + 1, 8, width), f32),
+        pltpu.VMEM((8 * blocks, width), f32),
+        pltpu.SMEM((held + ghosts + 1,), jnp.int32),
+        pltpu.SMEM((STEPS, 8, width), jnp.int32),
+        pltpu.VMEM((8, width), jnp.int32),
+        pltpu.VMEM((STEPS, 8, width), jnp.int32),
+        pltpu.VMEM((STEPS, 2, 2, 2, per_cell // 2, 8, width), f32),
+        pltpu.VMEM((STEPS, 6, 2, 2, per_cell // 2, 8, width), f32),
+        pltpu.VMEM((STEPS, 2, 2, 2, per_cell // 2, 8, width), f32),
+        pltpu.VMEM((STEPS, 6, 2, 2, per_cell // 2, 8, width), f32),
+        pltpu.VMEM((STEPS, 8 * capacity, width), f32),
+        pltpu.VMEM((STEPS, 8 * capacity, width), f32),
+        pltpu.VMEM((STEPS, 8 * capacity, width), f32),
+        pltpu.VMEM((STEPS, 8 * capacity, width), f32),
+        pltpu.VMEM((STEPS, 8 * capacity, width), f32),
+        pltpu.VMEM((STEPS, 8 * capacity, width), f32),
+        pltpu.VMEM((8 * capacity, width), f32),
+        pltpu.VMEM((8 * capacity, width), f32),
+        pltpu.VMEM((8 * capacity, width), f32),
+        pltpu.SemaphoreType.DMA((6,)),
+        pltpu.SemaphoreType.DMA,
+        pltpu.SemaphoreType.DMA((STEPS,)),
+        pltpu.SemaphoreType.DMA((STEPS,)),
+        pltpu.SemaphoreType.DMA((STEPS, 6)),
+        pltpu.SemaphoreType.DMA((STEPS, 6)),
+        pltpu.SemaphoreType.DMA((STEPS, 6)),
+        pltpu.SemaphoreType.DMA((STEPS, 6)),
+        pltpu.SemaphoreType.DMA((STEPS,)),
+        pltpu.SemaphoreType.DMA((STEPS,)),
+        pltpu.SemaphoreType.DMA((STEPS,)),
+        pltpu.SemaphoreType.DMA((STEPS,)),
+        pltpu.SemaphoreType.DMA((STEPS,)),
+        pltpu.SemaphoreType.DMA((STEPS,)),
+    ]
+    orders = [(0, 1, 2), (0, 2, 1), (1, 0, 2), (1, 2, 0), (2, 0, 1), (2, 1, 0)]
+
+    def with_order(number):
+        return pl.pallas_call(
+            functools.partial(kernel, (blocks, tiles, ghosts, capacity), orders[number]),
+            out_shape=jax.ShapeDtypeStruct((12 * blocks, width), f32),
+            in_specs=[vmem] + [smem] * 4 + [pl.BlockSpec(memory_space=pltpu.HBM)] * 2,
+            out_specs=vmem,
+            scratch_shapes=scratch,
+            compiler_params=pltpu.CompilerParams(
+                collective_id=number, has_side_effects=True, vmem_limit_bytes=63 * 1024 * 1024
+            ),
+        )
+
+    code = jnp.sum(cut_axis * jnp.maximum(3 - 2 * jnp.arange(STEPS, dtype=jnp.int32), 0))
+    number = code - 1 - lax.shift_right_logical(code, 2)
+    result = lax.switch(
+        number,
+        [with_order(k) for k in range(6)],
         pair_list[0].T,
         tile_count,
         ghost_list[0].T,
-        cut_axis,
         jnp.transpose(mig_list, (1, 0, 2)),
         mig_count,
         jnp.transpose(segments, (1, 0, 2)).reshape(12 * blocks, width),

time: 71.9 us -> 69.5 us (0.967)
  Pallas kernels: 69.1 us -> 64.5 us
  loops' own time: 0 us -> 0.76 us
    pallas_call x1, Pallas kernels: 69.1 us -> 64.5 us  [on_device(): lax.switch(number, [with_order(k) for k in range(6)], pair_list[0].T, til...]
    another operation x0 -> x1, loops' own time: none -> 0.76 us  [on_device(): lax.switch(number, [with_order(k) for k in range(6)], pair_list[0].T, til...]
    unnamed x1 -> x11, local copies, waits for them, and re-layouts: 1.77 us -> 2.1 us
where the time goes in v5:
time: 69.5 us; the launch traced here: 69.3 us
  Pallas kernels  64.5 us (93%)
  local copies, waits for them, and re-layouts  2.1 us (3%)
  between operations  1.34 us (2%)
  loops' own time  0.76 us (1%)
    pallas_call x1, Pallas kernels, on_device(): lax.switch(number, [with_order(k) for k in range(6)], pair_list[0].T, til...  64.5 us
    unnamed x11, local copies, waits for them, and re-layouts  2.1 us

profile of v5, /device:TPU:2, one launch (start us, length us, event | category | flops | bytes accessed | tf_op | source)
XLA Modules:
  0.0 69.3 jit_solution(15083783159374597080)
XLA Ops:
  0.0 0.0 copy-start.4
  0.0 0.7 copy-done.4
  0.7 0.6 multiply_reduce_fusion
  2.6 0.0 copy-start.3
  2.6 0.0 copy-start
  2.6 0.0 copy-start.1
  2.6 0.0 copy-start.2
  2.6 0.6 copy-done.3
  3.2 0.0 copy-done
  3.3 0.0 copy-done.1
  3.3 0.0 copy-done.2
  3.3 65.2 %conditional.1 = (f32[768,128]{1,0:T(8,128)S(1)}) conditional(s32[]{:T(128)} %clamp.3, (s32[2,512]{1,0:T(2,128)S(1)}, s32[1]{0:T(128)}, s32[4,8]{1,0:T(4,128)S(1)}, s32[3,1,24]{2,1,0:T(1,128)S(1)}, s32[1,3]{1,0:T(1,128)S(1)}, /*index=5*/f32[768,128]{1,0:T(8,128)}, f32[128,128]{1,0:T(8,128)}) %tuple.54, ...), branch_computations={%region_1.0_spmd, %region_2.0_spmd, %region_3.0_spmd, %region_4.0_... | conditional | bytes 8 | solution.py:614
  3.5 64.5 %branch_4_fun.1 = f32[768,128]{1,0:T(8,128)S(1)} custom-call(s32[2,512]{1,0:T(2,128)S(1)} %get-tuple-element.124.pairs, s32[1]{0:T(128)} %get-tuple-element.125.used, s32[4,8]{1,0:T(4,128)S(1)} %get-tuple-element.126.ghost_list, s32[3,1,24]{2,1,0:T(1,128)S(1)} %get-tuple-element.127.lists, s32[1,3]{1,0:T(1,128)S(1)} %get-tuple-element.128.amounts, ...), custom_call_target="tpu_custom_call" | custom-call | tf_op jit(solution)/shard_map/cond/branch_4_fun/pallas_call | solution.py:614
  68.5 0.7 %copy.16 = f32[64,12,128]{2,0,1:T(8,128)} copy(f32[64,12,128]{2,0,1:T(8,128)S(1)} %bitcast.19) | data formatting | bytes 786432
Async XLA Ops:
  0.0 0.7 copy-start.4
  2.6 0.7 copy-start.3
  2.6 0.7 %copy-start = (s32[1,512,2]{1,2,0:T(2,128)S(1)}, s32[1,512,2]{1,2,0:T(2,128)}, u32[]{:S(2)}) copy-start(s32[1,512,2]{1,2,0:T(2,128)} %param.17) | copy-start | bytes 12292
  2.6 0.7 copy-start.1
  2.6 0.7 copy-start.2
